TPU v7x, 32 devices: a whole 2x2x4 slice. The times are simulated.
32 devices in a mesh: groups: 2 (over x), seq: 16 (over z, y, core).
Axes of the slice: x: 2, y: 2, z: 4, core: 2. Of those that a mesh axis runs over, the one named last changes fastest.
Arguments:
- queries: bfloat16 [8192, 768], P(('groups', 'seq')), parts along dimension 0, may hold values from -10 to 10
- keys: bfloat16 [8192, 768], P(('groups', 'seq')), parts along dimension 0, may hold values from -10 to 10
- values: bfloat16 [8192, 768], P(('groups', 'seq')), parts along dimension 0, may hold values from -6 to 6
- grad_out: bfloat16 [8192, 768], P(('groups', 'seq')), parts along dimension 0, may hold values from -6 to 6
- local_span: int32 [16], replicated, may hold values from 64 to 256, as said below
- head_residue: int32 [16], replicated, may hold values from 0 to 15
- valid_count: int32 [2], P('groups'), parts along dimension 0, may hold values from 1024 to 4096
Outputs:
- query_gradient: bfloat16 [8192, 768], P(('groups', 'seq')), parts along dimension 0
- key_gradient: bfloat16 [8192, 768], P(('groups', 'seq')), parts along dimension 0
- value_gradient: bfloat16 [8192, 768], P(('groups', 'seq')), parts along dimension 0
There are 2 independent parts, one for each index of `groups`. A program takes and returns all parts, laid end to end along the dimension named above; an argument that names none is the same for every part. Nothing has to cross between parts.
Inputs may be any that keep to these rules, and one draw needn't show every extreme that they name: `local_span`: each head's local segment length is 256, 128 or 64; the longest and the shortest both occur. Positions from valid_count on are padding tiles.
All inputs are finite; a program needn't handle non-finite values.
Results may differ from a plain program's by a relative error of at most 0.0072.
Values may be sent and summed in bfloat16 or wider, within the bound.
A program may use at most 128 MiB of HBM per device.

v0:
```python
import math

import jax
import jax.numpy as jnp
from jax import lax
from jax.sharding import PartitionSpec as P

DILATION_STEP = 16
PARTS_IN_WINDOW = 16


SCORE_FLOOR = -1e30
PRECISE_MODE = lax.Precision.HIGHEST


def for_sending(x):
    return jax.tree.map(lambda a: a.astype(jnp.bfloat16) if a.dtype == jnp.float32 else a, x)


def shifted(block, axis, distance):
    devices = range(lax.axis_size(axis))
    route = [((i - distance) % len(devices), i) for i in devices]
    return lax.ppermute(block, axis, route)


def select_heads(tokens_heads, indicator_matrix):
    grouped = tokens_heads.reshape(
        tokens_heads.shape[0] // DILATION_STEP,
        DILATION_STEP,
        tokens_heads.shape[1],
        tokens_heads.shape[2],
    )
    return jnp.einsum("trhe,hr->the", grouped, indicator_matrix, preferred_element_type=jnp.float32)


def select_statistics(stats, indicator_matrix):
    grouped = stats.reshape(stats.shape[0] // DILATION_STEP, DILATION_STEP, stats.shape[1])
    return jnp.einsum("trh,hr->th", grouped, indicator_matrix, precision=PRECISE_MODE)


def distribute_heads(picked, indicator_matrix):
    full_rows = jnp.einsum("the,hr->trhe", picked, indicator_matrix, precision=PRECISE_MODE)
    return full_rows.reshape(-1, picked.shape[1], picked.shape[2])


def distribute_statistics(picked, indicator_matrix):
    full_rows = jnp.einsum("th,hr->trh", picked, indicator_matrix, precision=PRECISE_MODE)
    return full_rows.reshape(-1, picked.shape[1])


def local_mask(spans, key_valid):
    inner = jnp.arange(key_valid.shape[0], dtype=jnp.int32)
    segment_of = inner[None, :] // spans[:, None]
    return (segment_of[:, :, None] == segment_of[:, None, :]) & key_valid[None, None, :]


def shards(queries, keys, values, grad_out, local_span, head_residue, valid_count):
    patch_entries, hidden_width = queries.shape
    number_heads = local_span.shape[0]
    head_feature_width = hidden_width // number_heads
    score_scale = 1.0 / math.sqrt(head_feature_width)
    cycle_size = lax.axis_size("seq")
    circuit_position = lax.axis_index("seq")
    mask_count_total = valid_count[0]
    sparse_rows = patch_entries // DILATION_STEP
    query_per_head = queries.reshape(patch_entries, number_heads, head_feature_width)
    key_per_head = keys.reshape(patch_entries, number_heads, head_feature_width)
    value_per_head = values.reshape(patch_entries, number_heads, head_feature_width)
    output_gradient_heads = grad_out.reshape(patch_entries, number_heads, head_feature_width)
    indicator_matrix = (
        head_residue[:, None] == jnp.arange(DILATION_STEP, dtype=jnp.int32)[None, :]
    ).astype(jnp.float32)
    indicator_lowprec = indicator_matrix.astype(jnp.bfloat16)
    positions = circuit_position * patch_entries + jnp.arange(patch_entries, dtype=jnp.int32)
    row_mask = positions < mask_count_total
    shard_lanes = (
        jnp.arange(sparse_rows, dtype=jnp.int32)[:, None] * DILATION_STEP + head_residue[None, :]
    )
    sparse_row_mask = circuit_position * patch_entries + shard_lanes < mask_count_total
    thinned_probes = select_heads(query_per_head, indicator_lowprec).astype(jnp.bfloat16)
    sparse_keys = select_heads(key_per_head, indicator_lowprec).astype(jnp.bfloat16)
    sparse_values = select_heads(value_per_head, indicator_lowprec).astype(jnp.bfloat16)
    sparse_output_gradient = select_heads(output_gradient_heads, indicator_lowprec).astype(
        jnp.bfloat16
    )
    segment_id = circuit_position // PARTS_IN_WINDOW

    def key_mask(row_numbers):
        sender_shards = row_numbers // sparse_rows
        dense_rows = row_numbers % sparse_rows
        key_pos = (
            sender_shards[None, :] * patch_entries
            + dense_rows[None, :] * DILATION_STEP
            + head_residue[:, None]
        )
        key_ok = (key_pos < mask_count_total) & (
            sender_shards[None, :] // PARTS_IN_WINDOW == segment_id
        )
        return key_ok[:, None, :]

    def block_rows(sender_shard):
        return sender_shard * sparse_rows + jnp.arange(sparse_rows, dtype=jnp.int32)

    def protected_input(update, carried, sender_shard, lookup_patch_group, value_tile_block):
        allowed = key_mask(block_rows(sender_shard))
        return update(carried, allowed, lookup_patch_group, value_tile_block)

    def forward_merge_update(carried, allowed, lookup_patch_group, value_tile_block):
        running_maximum, row_count_total, running_total = carried
        scores = (
            jnp.einsum(
                "nij,bij->inb",
                thinned_probes,
                lookup_patch_group,
                preferred_element_type=jnp.float32,
            )
            * score_scale
        )
        new_largest = jnp.maximum(
            running_maximum, jnp.max(jnp.where(allowed, scores, SCORE_FLOOR), axis=2)
        )
        fading = jnp.exp(running_maximum - new_largest)
        weight = jnp.where(allowed, jnp.exp(scores - new_largest[:, :, None]), 0.0)
        row_count_total = row_count_total * fading + jnp.sum(weight, axis=2)
        running_total = running_total * fading[:, :, None] + jnp.einsum(
            "hab,bhe->hae", weight, value_tile_block.astype(jnp.float32), precision=PRECISE_MODE
        )
        return (new_largest, row_count_total, running_total)

    initial_state = (
        jnp.full((number_heads, sparse_rows), SCORE_FLOOR, jnp.float32),
        jnp.zeros((number_heads, sparse_rows), jnp.float32),
        jnp.zeros((number_heads, sparse_rows, head_feature_width), jnp.float32),
    )

    def source(hop_index):
        return (circuit_position - hop_index) % cycle_size

    loop_accumulator = protected_input(
        forward_merge_update, initial_state, circuit_position, sparse_keys, sparse_values
    )
    saved_keys = (
        jnp.zeros((cycle_size, sparse_rows, number_heads, head_feature_width), jnp.bfloat16)
        .at[0]
        .set(sparse_keys)
    )
    saved_values = (
        jnp.zeros((cycle_size, sparse_rows, number_heads, head_feature_width), jnp.bfloat16)
        .at[0]
        .set(sparse_values)
    )

    def forward_hop_step(hop_index, loop_state):
        blocks, carried, retained_lookups, kept_values = loop_state
        blocks = jax.tree.map(
            lambda part, own: part.astype(own.dtype), shifted(for_sending(blocks), "seq", 1), blocks
        )
        carried = protected_input(
            forward_merge_update, carried, source(hop_index), blocks[0], blocks[1]
        )
        retained_lookups = lax.dynamic_update_index_in_dim(
            retained_lookups, blocks[0], hop_index, 0
        )
        kept_values = lax.dynamic_update_index_in_dim(kept_values, blocks[1], hop_index, 0)
        return (blocks, carried, retained_lookups, kept_values)

    unused, loop_accumulator, saved_keys, saved_values = lax.fori_loop(
        1,
        cycle_size,
        forward_hop_step,
        ((sparse_keys, sparse_values), loop_accumulator, saved_keys, saved_values),
    )
    running_maximum, row_count_total, running_total = loop_accumulator
    sparse_column_mask = jnp.transpose(sparse_row_mask)
    sparse_logsumexp = running_maximum + jnp.log(
        row_count_total + 1.0 - sparse_column_mask.astype(jnp.float32)
    )
    group_size = max(number_heads // 4, 1)
    lse_parts = []
    for first_head in range(0, number_heads, group_size):
        heads_here = slice(first_head, first_head + group_size)
        allowed = local_mask(local_span[heads_here], row_mask)
        scores = (
            jnp.einsum(
                "ihe,jhe->hij",
                query_per_head[:, heads_here],
                key_per_head[:, heads_here],
                preferred_element_type=jnp.float32,
            )
            * score_scale
        )
        largest_here = jnp.max(jnp.where(allowed, scores, SCORE_FLOOR), axis=2)
        total_here = jnp.sum(
            jnp.where(allowed, jnp.exp(scores - largest_here[:, :, None]), 0.0), axis=2
        )
        lse_parts.append(
            largest_here + jnp.log(total_here + 1.0 - row_mask.astype(jnp.float32)[None, :])
        )
    dense_logsumexp = jnp.transpose(jnp.concatenate(lse_parts, axis=0))
    dense_sparse_logsumexp = select_statistics(dense_logsumexp, indicator_matrix)
    merged_output = jnp.where(
        sparse_row_mask, jnp.logaddexp(dense_sparse_logsumexp, jnp.transpose(sparse_logsumexp)), 0.0
    )
    complete_logsumexp = jnp.where(
        row_mask[:, None],
        dense_logsumexp
        + distribute_statistics(merged_output - dense_sparse_logsumexp, indicator_matrix),
        0.0,
    )
    global_scale = jnp.exp(running_maximum - jnp.transpose(merged_output))
    sparse_output = jnp.where(
        sparse_column_mask[:, :, None], running_total * global_scale[:, :, None], 0.0
    )
    global_output = distribute_heads(jnp.transpose(sparse_output, (1, 0, 2)), indicator_matrix)
    probe_derivative_pieces = []
    grad_k_parts = []
    grad_v_parts = []
    delta_parts = []
    for first_head in range(0, number_heads, group_size):
        heads_here = slice(first_head, first_head + group_size)
        query_here = query_per_head[:, heads_here]
        key_here = key_per_head[:, heads_here]
        value_here = value_per_head[:, heads_here]
        grad_here = output_gradient_heads[:, heads_here]
        allowed = local_mask(local_span[heads_here], row_mask) & row_mask[None, :, None]
        scores = (
            jnp.einsum("ihe,jhe->hij", query_here, key_here, preferred_element_type=jnp.float32)
            * score_scale
        )
        lse_here = jnp.transpose(complete_logsumexp[:, heads_here])
        weight = jnp.where(allowed, jnp.exp(scores - lse_here[:, :, None]), 0.0)
        weight_half = weight.astype(jnp.bfloat16)
        output = (
            jnp.einsum("hij,jhe->ihe", weight_half, value_here, preferred_element_type=jnp.float32)
            + global_output[:, heads_here]
        )
        delta_here = jnp.where(
            row_mask[:, None], jnp.sum(grad_here.astype(jnp.float32) * output, axis=2), 0.0
        )
        grad_v_parts.append(
            jnp.einsum("hij,ihe->jhe", weight_half, grad_here, preferred_element_type=jnp.float32)
        )
        dprod = jnp.einsum(
            "ihe,jhe->hij", grad_here, value_here, preferred_element_type=jnp.float32
        )
        logit_derivative = (weight * (dprod - jnp.transpose(delta_here)[:, :, None])).astype(
            jnp.bfloat16
        )
        probe_derivative_pieces.append(
            score_scale
            * jnp.einsum(
                "hij,jhe->ihe", logit_derivative, key_here, preferred_element_type=jnp.float32
            )
        )
        grad_k_parts.append(
            score_scale
            * jnp.einsum(
                "hij,ihe->jhe", logit_derivative, query_here, preferred_element_type=jnp.float32
            )
        )
        delta_parts.append(delta_here)
    dense_query_gradient = jnp.concatenate(probe_derivative_pieces, axis=1)
    dense_key_gradient = jnp.concatenate(grad_k_parts, axis=1)
    dense_value_gradient = jnp.concatenate(grad_v_parts, axis=1)
    row_delta = jnp.concatenate(delta_parts, axis=1)
    delta_t = jnp.transpose(select_statistics(row_delta, indicator_matrix))
    combined_t = jnp.transpose(merged_output)
    query_mask = sparse_column_mask[:, :, None]

    def backward_update(carried, allowed, lookup_patch_group, value_tile_block):
        grad_query, grad_key, grad_value = carried
        scores = (
            jnp.einsum(
                "nij,bij->inb",
                thinned_probes,
                lookup_patch_group,
                preferred_element_type=jnp.float32,
            )
            * score_scale
        )
        weight = jnp.where(allowed & query_mask, jnp.exp(scores - combined_t[:, :, None]), 0.0)
        grad_value = grad_value + jnp.einsum(
            "cwo,wcf->ocf",
            weight.astype(jnp.bfloat16),
            sparse_output_gradient,
            preferred_element_type=jnp.float32,
        )
        dprod = jnp.einsum(
            "nij,bij->inb",
            sparse_output_gradient,
            value_tile_block,
            preferred_element_type=jnp.float32,
        )
        logit_derivative = (weight * (dprod - delta_t[:, :, None])).astype(jnp.bfloat16)
        grad_query = grad_query + score_scale * jnp.einsum(
            "hab,bhe->ahe", logit_derivative, lookup_patch_group, preferred_element_type=jnp.float32
        )
        grad_key = grad_key + score_scale * jnp.einsum(
            "cwo,wcf->ocf", logit_derivative, thinned_probes, preferred_element_type=jnp.float32
        )
        return (grad_query, grad_key, grad_value)

    empty_block = jnp.zeros((sparse_rows, number_heads, head_feature_width), jnp.float32)

    def backward_step(hop_index, loop_state):
        grads_in, grad_query = loop_state
        lookup_patch_group = lax.dynamic_index_in_dim(saved_keys, hop_index, 0, keepdims=False)
        value_tile_block = lax.dynamic_index_in_dim(saved_values, hop_index, 0, keepdims=False)
        grad_query, grad_key, grad_value = protected_input(
            backward_update,
            (grad_query, grads_in[0], grads_in[1]),
            source(hop_index),
            lookup_patch_group,
            value_tile_block,
        )
        grads_out = (
            shifted(grad_key.astype(jnp.bfloat16), "seq", 1).astype(grad_key.dtype),
            shifted(grad_value.astype(jnp.bfloat16), "seq", 1).astype(grad_value.dtype),
        )
        return (grads_out, grad_query)

    gradient_triple, sparse_query_gradient = lax.fori_loop(
        0, cycle_size, backward_step, ((empty_block, empty_block), empty_block)
    )
    query_gradient = (
        (dense_query_gradient + distribute_heads(sparse_query_gradient, indicator_matrix))
        .astype(jnp.bfloat16)
        .reshape(patch_entries, hidden_width)
    )
    key_gradient = (
        (dense_key_gradient + distribute_heads(gradient_triple[0], indicator_matrix))
        .astype(jnp.bfloat16)
        .reshape(patch_entries, hidden_width)
    )
    value_gradient = (
        (dense_value_gradient + distribute_heads(gradient_triple[1], indicator_matrix))
        .astype(jnp.bfloat16)
        .reshape(patch_entries, hidden_width)
    )
    return (query_gradient, key_gradient, value_gradient)


def solution(mesh):
    return jax.shard_map(
        shards,
        mesh=mesh,
        in_specs=(
            P(("groups", "seq"), None),
            P(("groups", "seq"), None),
            P(("groups", "seq"), None),
            P(("groups", "seq"), None),
            P(),
            P(),
            P("groups"),
        ),
        out_specs=(
            P(("groups", "seq"), None),
            P(("groups", "seq"), None),
            P(("groups", "seq"), None),
        ),
        check_vma=False,
    )
```

profile of v0, /device:TPU:0, one launch (start us, length us, event | category | flops | bytes accessed | tf_op | source)
XLA Modules:
  0.0 424.0 jit_solution(557387648857844112)
XLA Ops:
  11.5 2.1 copy.70
  15.4 2.2 reshape_reshape.14
  18.0 2.2 reshape_reshape.12
  22.6 2.2 reshape_reshape.13
  26.9 148.7 %while.63 = (s32[]{:T(128)}, bf16[16,16,48]{2,0,1:T(8,128)(2,1)}, bf16[16,16,48]{2,0,1:T(8,128)(2,1)S(1)}, f32[16,16]{1,0:T(8,128)S(1)}, f32[16,16]{1,0:T(8,128)...) while((s32[]{:T(128)}, bf16[16,16,48]{2,0,1:T(8,128)(2,1)}, ...), condition=%wide.region_13.15_spmd, body=%wide.region_10.14_spmd.sunk | while | flops 2812034 | bytes 714396 | solution.py:167
  27.3 2.6 collective-permute-start
  30.7 4.3 %collective-permute-done = bf16[16,16,48]{2,0,1:T(8,128)(2,1)S(1)} collective-permute-done((bf16[16,16,48]{2,0,1:T(8,128)(2,1)}, bf16[16,16,48]{2,0,1:T(8,128)(2,1)S(1)}, u32[]{:S(2)}, u32[]{:S(2)}) %collective-permute-start) | collective-permute-done | bytes 24608 | tf_op jit(solution)/shard_map/while/body/eval_jaxpr/ppermute | solution.py:23
  38.6 6.2 %collective-permute-done = bf16[16,16,48]{2,0,1:T(8,128)(2,1)S(1)} collective-permute-done((bf16[16,16,48]{2,0,1:T(8,128)(2,1)}, bf16[16,16,48]{2,0,1:T(8,128)(2,1)S(1)}, u32[]{:S(2)}, u32[]{:S(2)}) %collective-permute-start) | collective-permute-done | bytes 24608 | tf_op jit(solution)/shard_map/while/body/eval_jaxpr/ppermute | solution.py:23
  48.5 6.2 %collective-permute-done = bf16[16,16,48]{2,0,1:T(8,128)(2,1)S(1)} collective-permute-done((bf16[16,16,48]{2,0,1:T(8,128)(2,1)}, bf16[16,16,48]{2,0,1:T(8,128)(2,1)S(1)}, u32[]{:S(2)}, u32[]{:S(2)}) %collective-permute-start) | collective-permute-done | bytes 24608 | tf_op jit(solution)/shard_map/while/body/eval_jaxpr/ppermute | solution.py:23
  58.3 6.2 %collective-permute-done = bf16[16,16,48]{2,0,1:T(8,128)(2,1)S(1)} collective-permute-done((bf16[16,16,48]{2,0,1:T(8,128)(2,1)}, bf16[16,16,48]{2,0,1:T(8,128)(2,1)S(1)}, u32[]{:S(2)}, u32[]{:S(2)}) %collective-permute-start) | collective-permute-done | bytes 24608 | tf_op jit(solution)/shard_map/while/body/eval_jaxpr/ppermute | solution.py:23
  68.1 6.2 %collective-permute-done = bf16[16,16,48]{2,0,1:T(8,128)(2,1)S(1)} collective-permute-done((bf16[16,16,48]{2,0,1:T(8,128)(2,1)}, bf16[16,16,48]{2,0,1:T(8,128)(2,1)S(1)}, u32[]{:S(2)}, u32[]{:S(2)}) %collective-permute-start) | collective-permute-done | bytes 24608 | tf_op jit(solution)/shard_map/while/body/eval_jaxpr/ppermute | solution.py:23
  78.0 6.2 %collective-permute-done = bf16[16,16,48]{2,0,1:T(8,128)(2,1)S(1)} collective-permute-done((bf16[16,16,48]{2,0,1:T(8,128)(2,1)}, bf16[16,16,48]{2,0,1:T(8,128)(2,1)S(1)}, u32[]{:S(2)}, u32[]{:S(2)}) %collective-permute-start) | collective-permute-done | bytes 24608 | tf_op jit(solution)/shard_map/while/body/eval_jaxpr/ppermute | solution.py:23
  87.8 6.2 %collective-permute-done = bf16[16,16,48]{2,0,1:T(8,128)(2,1)S(1)} collective-permute-done((bf16[16,16,48]{2,0,1:T(8,128)(2,1)}, bf16[16,16,48]{2,0,1:T(8,128)(2,1)S(1)}, u32[]{:S(2)}, u32[]{:S(2)}) %collective-permute-start) | collective-permute-done | bytes 24608 | tf_op jit(solution)/shard_map/while/body/eval_jaxpr/ppermute | solution.py:23
  97.7 6.2 %collective-permute-done = bf16[16,16,48]{2,0,1:T(8,128)(2,1)S(1)} collective-permute-done((bf16[16,16,48]{2,0,1:T(8,128)(2,1)}, bf16[16,16,48]{2,0,1:T(8,128)(2,1)S(1)}, u32[]{:S(2)}, u32[]{:S(2)}) %collective-permute-start) | collective-permute-done | bytes 24608 | tf_op jit(solution)/shard_map/while/body/eval_jaxpr/ppermute | solution.py:23
  107.5 6.2 %collective-permute-done = bf16[16,16,48]{2,0,1:T(8,128)(2,1)S(1)} collective-permute-done((bf16[16,16,48]{2,0,1:T(8,128)(2,1)}, bf16[16,16,48]{2,0,1:T(8,128)(2,1)S(1)}, u32[]{:S(2)}, u32[]{:S(2)}) %collective-permute-start) | collective-permute-done | bytes 24608 | tf_op jit(solution)/shard_map/while/body/eval_jaxpr/ppermute | solution.py:23
  117.4 6.2 %collective-permute-done = bf16[16,16,48]{2,0,1:T(8,128)(2,1)S(1)} collective-permute-done((bf16[16,16,48]{2,0,1:T(8,128)(2,1)}, bf16[16,16,48]{2,0,1:T(8,128)(2,1)S(1)}, u32[]{:S(2)}, u32[]{:S(2)}) %collective-permute-start) | collective-permute-done | bytes 24608 | tf_op jit(solution)/shard_map/while/body/eval_jaxpr/ppermute | solution.py:23
  127.2 6.2 %collective-permute-done = bf16[16,16,48]{2,0,1:T(8,128)(2,1)S(1)} collective-permute-done((bf16[16,16,48]{2,0,1:T(8,128)(2,1)}, bf16[16,16,48]{2,0,1:T(8,128)(2,1)S(1)}, u32[]{:S(2)}, u32[]{:S(2)}) %collective-permute-start) | collective-permute-done | bytes 24608 | tf_op jit(solution)/shard_map/while/body/eval_jaxpr/ppermute | solution.py:23
  137.1 6.2 %collective-permute-done = bf16[16,16,48]{2,0,1:T(8,128)(2,1)S(1)} collective-permute-done((bf16[16,16,48]{2,0,1:T(8,128)(2,1)}, bf16[16,16,48]{2,0,1:T(8,128)(2,1)S(1)}, u32[]{:S(2)}, u32[]{:S(2)}) %collective-permute-start) | collective-permute-done | bytes 24608 | tf_op jit(solution)/shard_map/while/body/eval_jaxpr/ppermute | solution.py:23
  147.0 6.2 %collective-permute-done = bf16[16,16,48]{2,0,1:T(8,128)(2,1)S(1)} collective-permute-done((bf16[16,16,48]{2,0,1:T(8,128)(2,1)}, bf16[16,16,48]{2,0,1:T(8,128)(2,1)S(1)}, u32[]{:S(2)}, u32[]{:S(2)}) %collective-permute-start) | collective-permute-done | bytes 24608 | tf_op jit(solution)/shard_map/while/body/eval_jaxpr/ppermute | solution.py:23
  156.8 6.2 %collective-permute-done = bf16[16,16,48]{2,0,1:T(8,128)(2,1)S(1)} collective-permute-done((bf16[16,16,48]{2,0,1:T(8,128)(2,1)}, bf16[16,16,48]{2,0,1:T(8,128)(2,1)S(1)}, u32[]{:S(2)}, u32[]{:S(2)}) %collective-permute-start) | collective-permute-done | bytes 24608 | tf_op jit(solution)/shard_map/while/body/eval_jaxpr/ppermute | solution.py:23
  166.7 6.2 %collective-permute-done = bf16[16,16,48]{2,0,1:T(8,128)(2,1)S(1)} collective-permute-done((bf16[16,16,48]{2,0,1:T(8,128)(2,1)}, bf16[16,16,48]{2,0,1:T(8,128)(2,1)S(1)}, u32[]{:S(2)}, u32[]{:S(2)}) %collective-permute-start) | collective-permute-done | bytes 24608 | tf_op jit(solution)/shard_map/while/body/eval_jaxpr/ppermute | solution.py:23
  176.9 2.2 reshape_reshape.15
  179.6 2.0 select_reduce_fusion.8
  181.7 2.3 select_reduce_fusion.7
  213.3 3.5 fusion.76
  220.0 2.3 copy.105
  222.3 2.7 fusion.45
  228.8 173.8 %while.64 = (s32[]{:T(128)}, f32[16,16,48]{2,0,1:T(8,128)S(1)}, f32[16,16,48]{2,0,1:T(8,128)S(1)}, f32[16,16,48]{2,0,1:T(8,128)S(1)}, s32[]{:T(128)}, /*index=5*...) while((s32[]{:T(128)}, f32[16,16,48]{2,0,1:T(8,128)S(1)}, ...), condition=%wide.region_19.21_spmd.clone.clone.clone, body=%wide.region_18.20_spmd.clone.clone.clone.sunk | while | flops 2148736 | bytes 963854 | solution.py:322
  234.0 5.1 %collective-permute-done.2 = bf16[16,16,48]{2,0,1:T(8,128)(2,1)S(1)} collective-permute-done((bf16[16,16,48]{2,0,1:T(8,128)(2,1)S(1)}, bf16[16,16,48]{2,0,1:T(8,128)(2,1)S(1)}, u32[]{:S(2)}, u32[]{:S(2)}) %collective-permute-start.2) | collective-permute-done | bytes 24608 | tf_op jit(solution)/shard_map/while/body/eval_jaxpr/ppermute | solution.py:23
  244.8 5.1 %collective-permute-done.2 = bf16[16,16,48]{2,0,1:T(8,128)(2,1)S(1)} collective-permute-done((bf16[16,16,48]{2,0,1:T(8,128)(2,1)S(1)}, bf16[16,16,48]{2,0,1:T(8,128)(2,1)S(1)}, u32[]{:S(2)}, u32[]{:S(2)}) %collective-permute-start.2) | collective-permute-done | bytes 24608 | tf_op jit(solution)/shard_map/while/body/eval_jaxpr/ppermute | solution.py:23
  255.7 5.1 %collective-permute-done.2 = bf16[16,16,48]{2,0,1:T(8,128)(2,1)S(1)} collective-permute-done((bf16[16,16,48]{2,0,1:T(8,128)(2,1)S(1)}, bf16[16,16,48]{2,0,1:T(8,128)(2,1)S(1)}, u32[]{:S(2)}, u32[]{:S(2)}) %collective-permute-start.2) | collective-permute-done | bytes 24608 | tf_op jit(solution)/shard_map/while/body/eval_jaxpr/ppermute | solution.py:23
  266.5 5.1 %collective-permute-done.2 = bf16[16,16,48]{2,0,1:T(8,128)(2,1)S(1)} collective-permute-done((bf16[16,16,48]{2,0,1:T(8,128)(2,1)S(1)}, bf16[16,16,48]{2,0,1:T(8,128)(2,1)S(1)}, u32[]{:S(2)}, u32[]{:S(2)}) %collective-permute-start.2) | collective-permute-done | bytes 24608 | tf_op jit(solution)/shard_map/while/body/eval_jaxpr/ppermute | solution.py:23
  277.4 5.1 %collective-permute-done.2 = bf16[16,16,48]{2,0,1:T(8,128)(2,1)S(1)} collective-permute-done((bf16[16,16,48]{2,0,1:T(8,128)(2,1)S(1)}, bf16[16,16,48]{2,0,1:T(8,128)(2,1)S(1)}, u32[]{:S(2)}, u32[]{:S(2)}) %collective-permute-start.2) | collective-permute-done | bytes 24608 | tf_op jit(solution)/shard_map/while/body/eval_jaxpr/ppermute | solution.py:23
  288.2 5.1 %collective-permute-done.2 = bf16[16,16,48]{2,0,1:T(8,128)(2,1)S(1)} collective-permute-done((bf16[16,16,48]{2,0,1:T(8,128)(2,1)S(1)}, bf16[16,16,48]{2,0,1:T(8,128)(2,1)S(1)}, u32[]{:S(2)}, u32[]{:S(2)}) %collective-permute-start.2) | collective-permute-done | bytes 24608 | tf_op jit(solution)/shard_map/while/body/eval_jaxpr/ppermute | solution.py:23
  299.1 5.1 %collective-permute-done.2 = bf16[16,16,48]{2,0,1:T(8,128)(2,1)S(1)} collective-permute-done((bf16[16,16,48]{2,0,1:T(8,128)(2,1)S(1)}, bf16[16,16,48]{2,0,1:T(8,128)(2,1)S(1)}, u32[]{:S(2)}, u32[]{:S(2)}) %collective-permute-start.2) | collective-permute-done | bytes 24608 | tf_op jit(solution)/shard_map/while/body/eval_jaxpr/ppermute | solution.py:23
  310.0 5.1 %collective-permute-done.2 = bf16[16,16,48]{2,0,1:T(8,128)(2,1)S(1)} collective-permute-done((bf16[16,16,48]{2,0,1:T(8,128)(2,1)S(1)}, bf16[16,16,48]{2,0,1:T(8,128)(2,1)S(1)}, u32[]{:S(2)}, u32[]{:S(2)}) %collective-permute-start.2) | collective-permute-done | bytes 24608 | tf_op jit(solution)/shard_map/while/body/eval_jaxpr/ppermute | solution.py:23
  320.8 5.1 %collective-permute-done.2 = bf16[16,16,48]{2,0,1:T(8,128)(2,1)S(1)} collective-permute-done((bf16[16,16,48]{2,0,1:T(8,128)(2,1)S(1)}, bf16[16,16,48]{2,0,1:T(8,128)(2,1)S(1)}, u32[]{:S(2)}, u32[]{:S(2)}) %collective-permute-start.2) | collective-permute-done | bytes 24608 | tf_op jit(solution)/shard_map/while/body/eval_jaxpr/ppermute | solution.py:23
  331.7 5.1 %collective-permute-done.2 = bf16[16,16,48]{2,0,1:T(8,128)(2,1)S(1)} collective-permute-done((bf16[16,16,48]{2,0,1:T(8,128)(2,1)S(1)}, bf16[16,16,48]{2,0,1:T(8,128)(2,1)S(1)}, u32[]{:S(2)}, u32[]{:S(2)}) %collective-permute-start.2) | collective-permute-done | bytes 24608 | tf_op jit(solution)/shard_map/while/body/eval_jaxpr/ppermute | solution.py:23
  342.5 5.1 %collective-permute-done.2 = bf16[16,16,48]{2,0,1:T(8,128)(2,1)S(1)} collective-permute-done((bf16[16,16,48]{2,0,1:T(8,128)(2,1)S(1)}, bf16[16,16,48]{2,0,1:T(8,128)(2,1)S(1)}, u32[]{:S(2)}, u32[]{:S(2)}) %collective-permute-start.2) | collective-permute-done | bytes 24608 | tf_op jit(solution)/shard_map/while/body/eval_jaxpr/ppermute | solution.py:23
  353.4 5.1 %collective-permute-done.2 = bf16[16,16,48]{2,0,1:T(8,128)(2,1)S(1)} collective-permute-done((bf16[16,16,48]{2,0,1:T(8,128)(2,1)S(1)}, bf16[16,16,48]{2,0,1:T(8,128)(2,1)S(1)}, u32[]{:S(2)}, u32[]{:S(2)}) %collective-permute-start.2) | collective-permute-done | bytes 24608 | tf_op jit(solution)/shard_map/while/body/eval_jaxpr/ppermute | solution.py:23
  364.3 5.1 %collective-permute-done.2 = bf16[16,16,48]{2,0,1:T(8,128)(2,1)S(1)} collective-permute-done((bf16[16,16,48]{2,0,1:T(8,128)(2,1)S(1)}, bf16[16,16,48]{2,0,1:T(8,128)(2,1)S(1)}, u32[]{:S(2)}, u32[]{:S(2)}) %collective-permute-start.2) | collective-permute-done | bytes 24608 | tf_op jit(solution)/shard_map/while/body/eval_jaxpr/ppermute | solution.py:23
  375.1 5.1 %collective-permute-done.2 = bf16[16,16,48]{2,0,1:T(8,128)(2,1)S(1)} collective-permute-done((bf16[16,16,48]{2,0,1:T(8,128)(2,1)S(1)}, bf16[16,16,48]{2,0,1:T(8,128)(2,1)S(1)}, u32[]{:S(2)}, u32[]{:S(2)}) %collective-permute-start.2) | collective-permute-done | bytes 24608 | tf_op jit(solution)/shard_map/while/body/eval_jaxpr/ppermute | solution.py:23
  386.0 5.1 %collective-permute-done.2 = bf16[16,16,48]{2,0,1:T(8,128)(2,1)S(1)} collective-permute-done((bf16[16,16,48]{2,0,1:T(8,128)(2,1)S(1)}, bf16[16,16,48]{2,0,1:T(8,128)(2,1)S(1)}, u32[]{:S(2)}, u32[]{:S(2)}) %collective-permute-start.2) | collective-permute-done | bytes 24608 | tf_op jit(solution)/shard_map/while/body/eval_jaxpr/ppermute | solution.py:23
  396.8 5.1 %collective-permute-done.2 = bf16[16,16,48]{2,0,1:T(8,128)(2,1)S(1)} collective-permute-done((bf16[16,16,48]{2,0,1:T(8,128)(2,1)S(1)}, bf16[16,16,48]{2,0,1:T(8,128)(2,1)S(1)}, u32[]{:S(2)}, u32[]{:S(2)}) %collective-permute-start.2) | collective-permute-done | bytes 24608 | tf_op jit(solution)/shard_map/while/body/eval_jaxpr/ppermute | solution.py:23
  407.3 2.8 multiply_bitcast_fusion
  410.1 3.1 reshape.601
  413.2 2.0 add_convert_fusion
  415.2 3.1 reshape.600
  (678 shorter events, 208.5 us)
Async XLA Ops:
  26.9 9.1 %collective-permute-start.1 = (bf16[16,16,48]{2,0,1:T(8,128)(2,1)S(1)}, bf16[16,16,48]{2,0,1:T(8,128)(2,1)S(1)}, u32[]{:S(2)}, u32[]{:S(2)}) collective-permute-start(bf16[16,16,48]{2,0,1:T(8,128)(2,1)S(1)} %get-tuple-element.1351), channel_id=1, source_target_pairs={{15,0},{0,1},{1,2},{2,3},{3,4},{4,5},{5,6},{6,7},{7,8},{8,9},{9,10... | collective-permute-start | bytes 73736 | tf_op jit(solution)/shard_map/while/body/eval_jaxpr/ppermute | solution.py:23
  27.3 7.6 %collective-permute-start = (bf16[16,16,48]{2,0,1:T(8,128)(2,1)}, bf16[16,16,48]{2,0,1:T(8,128)(2,1)S(1)}, u32[]{:S(2)}, u32[]{:S(2)}) collective-permute-start(bf16[16,16,48]{2,0,1:T(8,128)(2,1)} %get-tuple-element.1350), channel_id=1, source_target_pairs={{15,0},{0,1},{1,2},{2,3},{3,4},{4,5},{5,6},{6,7},{7,8},{8,9},{9,10... | collective-permute-start | bytes 73736 | tf_op jit(solution)/shard_map/while/body/eval_jaxpr/ppermute | solution.py:23
  37.7 8.1 %collective-permute-start.1 = (bf16[16,16,48]{2,0,1:T(8,128)(2,1)S(1)}, bf16[16,16,48]{2,0,1:T(8,128)(2,1)S(1)}, u32[]{:S(2)}, u32[]{:S(2)}) collective-permute-start(bf16[16,16,48]{2,0,1:T(8,128)(2,1)S(1)} %get-tuple-element.1351), channel_id=1, source_target_pairs={{15,0},{0,1},{1,2},{2,3},{3,4},{4,5},{5,6},{6,7},{7,8},{8,9},{9,10... | collective-permute-start | bytes 73736 | tf_op jit(solution)/shard_map/while/body/eval_jaxpr/ppermute | solution.py:23
  37.7 7.1 %collective-permute-start = (bf16[16,16,48]{2,0,1:T(8,128)(2,1)}, bf16[16,16,48]{2,0,1:T(8,128)(2,1)S(1)}, u32[]{:S(2)}, u32[]{:S(2)}) collective-permute-start(bf16[16,16,48]{2,0,1:T(8,128)(2,1)} %get-tuple-element.1350), channel_id=1, source_target_pairs={{15,0},{0,1},{1,2},{2,3},{3,4},{4,5},{5,6},{6,7},{7,8},{8,9},{9,10... | collective-permute-start | bytes 73736 | tf_op jit(solution)/shard_map/while/body/eval_jaxpr/ppermute | solution.py:23
  47.5 8.1 %collective-permute-start.1 = (bf16[16,16,48]{2,0,1:T(8,128)(2,1)S(1)}, bf16[16,16,48]{2,0,1:T(8,128)(2,1)S(1)}, u32[]{:S(2)}, u32[]{:S(2)}) collective-permute-start(bf16[16,16,48]{2,0,1:T(8,128)(2,1)S(1)} %get-tuple-element.1351), channel_id=1, source_target_pairs={{15,0},{0,1},{1,2},{2,3},{3,4},{4,5},{5,6},{6,7},{7,8},{8,9},{9,10... | collective-permute-start | bytes 73736 | tf_op jit(solution)/shard_map/while/body/eval_jaxpr/ppermute | solution.py:23
  47.6 7.1 %collective-permute-start = (bf16[16,16,48]{2,0,1:T(8,128)(2,1)}, bf16[16,16,48]{2,0,1:T(8,128)(2,1)S(1)}, u32[]{:S(2)}, u32[]{:S(2)}) collective-permute-start(bf16[16,16,48]{2,0,1:T(8,128)(2,1)} %get-tuple-element.1350), channel_id=1, source_target_pairs={{15,0},{0,1},{1,2},{2,3},{3,4},{4,5},{5,6},{6,7},{7,8},{8,9},{9,10... | collective-permute-start | bytes 73736 | tf_op jit(solution)/shard_map/while/body/eval_jaxpr/ppermute | solution.py:23
  57.4 8.1 %collective-permute-start.1 = (bf16[16,16,48]{2,0,1:T(8,128)(2,1)S(1)}, bf16[16,16,48]{2,0,1:T(8,128)(2,1)S(1)}, u32[]{:S(2)}, u32[]{:S(2)}) collective-permute-start(bf16[16,16,48]{2,0,1:T(8,128)(2,1)S(1)} %get-tuple-element.1351), channel_id=1, source_target_pairs={{15,0},{0,1},{1,2},{2,3},{3,4},{4,5},{5,6},{6,7},{7,8},{8,9},{9,10... | collective-permute-start | bytes 73736 | tf_op jit(solution)/shard_map/while/body/eval_jaxpr/ppermute | solution.py:23
  57.4 7.1 %collective-permute-start = (bf16[16,16,48]{2,0,1:T(8,128)(2,1)}, bf16[16,16,48]{2,0,1:T(8,128)(2,1)S(1)}, u32[]{:S(2)}, u32[]{:S(2)}) collective-permute-start(bf16[16,16,48]{2,0,1:T(8,128)(2,1)} %get-tuple-element.1350), channel_id=1, source_target_pairs={{15,0},{0,1},{1,2},{2,3},{3,4},{4,5},{5,6},{6,7},{7,8},{8,9},{9,10... | collective-permute-start | bytes 73736 | tf_op jit(solution)/shard_map/while/body/eval_jaxpr/ppermute | solution.py:23
  67.2 8.1 %collective-permute-start.1 = (bf16[16,16,48]{2,0,1:T(8,128)(2,1)S(1)}, bf16[16,16,48]{2,0,1:T(8,128)(2,1)S(1)}, u32[]{:S(2)}, u32[]{:S(2)}) collective-permute-start(bf16[16,16,48]{2,0,1:T(8,128)(2,1)S(1)} %get-tuple-element.1351), channel_id=1, source_target_pairs={{15,0},{0,1},{1,2},{2,3},{3,4},{4,5},{5,6},{6,7},{7,8},{8,9},{9,10... | collective-permute-start | bytes 73736 | tf_op jit(solution)/shard_map/while/body/eval_jaxpr/ppermute | solution.py:23
  67.3 7.1 %collective-permute-start = (bf16[16,16,48]{2,0,1:T(8,128)(2,1)}, bf16[16,16,48]{2,0,1:T(8,128)(2,1)S(1)}, u32[]{:S(2)}, u32[]{:S(2)}) collective-permute-start(bf16[16,16,48]{2,0,1:T(8,128)(2,1)} %get-tuple-element.1350), channel_id=1, source_target_pairs={{15,0},{0,1},{1,2},{2,3},{3,4},{4,5},{5,6},{6,7},{7,8},{8,9},{9,10... | collective-permute-start | bytes 73736 | tf_op jit(solution)/shard_map/while/body/eval_jaxpr/ppermute | solution.py:23
  77.1 8.1 %collective-permute-start.1 = (bf16[16,16,48]{2,0,1:T(8,128)(2,1)S(1)}, bf16[16,16,48]{2,0,1:T(8,128)(2,1)S(1)}, u32[]{:S(2)}, u32[]{:S(2)}) collective-permute-start(bf16[16,16,48]{2,0,1:T(8,128)(2,1)S(1)} %get-tuple-element.1351), channel_id=1, source_target_pairs={{15,0},{0,1},{1,2},{2,3},{3,4},{4,5},{5,6},{6,7},{7,8},{8,9},{9,10... | collective-permute-start | bytes 73736 | tf_op jit(solution)/shard_map/while/body/eval_jaxpr/ppermute | solution.py:23
  77.1 7.1 %collective-permute-start = (bf16[16,16,48]{2,0,1:T(8,128)(2,1)}, bf16[16,16,48]{2,0,1:T(8,128)(2,1)S(1)}, u32[]{:S(2)}, u32[]{:S(2)}) collective-permute-start(bf16[16,16,48]{2,0,1:T(8,128)(2,1)} %get-tuple-element.1350), channel_id=1, source_target_pairs={{15,0},{0,1},{1,2},{2,3},{3,4},{4,5},{5,6},{6,7},{7,8},{8,9},{9,10... | collective-permute-start | bytes 73736 | tf_op jit(solution)/shard_map/while/body/eval_jaxpr/ppermute | solution.py:23
  86.9 8.1 %collective-permute-start.1 = (bf16[16,16,48]{2,0,1:T(8,128)(2,1)S(1)}, bf16[16,16,48]{2,0,1:T(8,128)(2,1)S(1)}, u32[]{:S(2)}, u32[]{:S(2)}) collective-permute-start(bf16[16,16,48]{2,0,1:T(8,128)(2,1)S(1)} %get-tuple-element.1351), channel_id=1, source_target_pairs={{15,0},{0,1},{1,2},{2,3},{3,4},{4,5},{5,6},{6,7},{7,8},{8,9},{9,10... | collective-permute-start | bytes 73736 | tf_op jit(solution)/shard_map/while/body/eval_jaxpr/ppermute | solution.py:23
  87.0 7.1 %collective-permute-start = (bf16[16,16,48]{2,0,1:T(8,128)(2,1)}, bf16[16,16,48]{2,0,1:T(8,128)(2,1)S(1)}, u32[]{:S(2)}, u32[]{:S(2)}) collective-permute-start(bf16[16,16,48]{2,0,1:T(8,128)(2,1)} %get-tuple-element.1350), channel_id=1, source_target_pairs={{15,0},{0,1},{1,2},{2,3},{3,4},{4,5},{5,6},{6,7},{7,8},{8,9},{9,10... | collective-permute-start | bytes 73736 | tf_op jit(solution)/shard_map/while/body/eval_jaxpr/ppermute | solution.py:23
  96.8 8.1 %collective-permute-start.1 = (bf16[16,16,48]{2,0,1:T(8,128)(2,1)S(1)}, bf16[16,16,48]{2,0,1:T(8,128)(2,1)S(1)}, u32[]{:S(2)}, u32[]{:S(2)}) collective-permute-start(bf16[16,16,48]{2,0,1:T(8,128)(2,1)S(1)} %get-tuple-element.1351), channel_id=1, source_target_pairs={{15,0},{0,1},{1,2},{2,3},{3,4},{4,5},{5,6},{6,7},{7,8},{8,9},{9,10... | collective-permute-start | bytes 73736 | tf_op jit(solution)/shard_map/while/body/eval_jaxpr/ppermute | solution.py:23
  96.9 7.1 %collective-permute-start = (bf16[16,16,48]{2,0,1:T(8,128)(2,1)}, bf16[16,16,48]{2,0,1:T(8,128)(2,1)S(1)}, u32[]{:S(2)}, u32[]{:S(2)}) collective-permute-start(bf16[16,16,48]{2,0,1:T(8,128)(2,1)} %get-tuple-element.1350), channel_id=1, source_target_pairs={{15,0},{0,1},{1,2},{2,3},{3,4},{4,5},{5,6},{6,7},{7,8},{8,9},{9,10... | collective-permute-start | bytes 73736 | tf_op jit(solution)/shard_map/while/body/eval_jaxpr/ppermute | solution.py:23
  106.6 8.1 %collective-permute-start.1 = (bf16[16,16,48]{2,0,1:T(8,128)(2,1)S(1)}, bf16[16,16,48]{2,0,1:T(8,128)(2,1)S(1)}, u32[]{:S(2)}, u32[]{:S(2)}) collective-permute-start(bf16[16,16,48]{2,0,1:T(8,128)(2,1)S(1)} %get-tuple-element.1351), channel_id=1, source_target_pairs={{15,0},{0,1},{1,2},{2,3},{3,4},{4,5},{5,6},{6,7},{7,8},{8,9},{9,10... | collective-permute-start | bytes 73736 | tf_op jit(solution)/shard_map/while/body/eval_jaxpr/ppermute | solution.py:23
  106.7 7.1 %collective-permute-start = (bf16[16,16,48]{2,0,1:T(8,128)(2,1)}, bf16[16,16,48]{2,0,1:T(8,128)(2,1)S(1)}, u32[]{:S(2)}, u32[]{:S(2)}) collective-permute-start(bf16[16,16,48]{2,0,1:T(8,128)(2,1)} %get-tuple-element.1350), channel_id=1, source_target_pairs={{15,0},{0,1},{1,2},{2,3},{3,4},{4,5},{5,6},{6,7},{7,8},{8,9},{9,10... | collective-permute-start | bytes 73736 | tf_op jit(solution)/shard_map/while/body/eval_jaxpr/ppermute | solution.py:23
  116.5 8.1 %collective-permute-start.1 = (bf16[16,16,48]{2,0,1:T(8,128)(2,1)S(1)}, bf16[16,16,48]{2,0,1:T(8,128)(2,1)S(1)}, u32[]{:S(2)}, u32[]{:S(2)}) collective-permute-start(bf16[16,16,48]{2,0,1:T(8,128)(2,1)S(1)} %get-tuple-element.1351), channel_id=1, source_target_pairs={{15,0},{0,1},{1,2},{2,3},{3,4},{4,5},{5,6},{6,7},{7,8},{8,9},{9,10... | collective-permute-start | bytes 73736 | tf_op jit(solution)/shard_map/while/body/eval_jaxpr/ppermute | solution.py:23
  116.5 7.1 %collective-permute-start = (bf16[16,16,48]{2,0,1:T(8,128)(2,1)}, bf16[16,16,48]{2,0,1:T(8,128)(2,1)S(1)}, u32[]{:S(2)}, u32[]{:S(2)}) collective-permute-start(bf16[16,16,48]{2,0,1:T(8,128)(2,1)} %get-tuple-element.1350), channel_id=1, source_target_pairs={{15,0},{0,1},{1,2},{2,3},{3,4},{4,5},{5,6},{6,7},{7,8},{8,9},{9,10... | collective-permute-start | bytes 73736 | tf_op jit(solution)/shard_map/while/body/eval_jaxpr/ppermute | solution.py:23
  126.3 8.1 %collective-permute-start.1 = (bf16[16,16,48]{2,0,1:T(8,128)(2,1)S(1)}, bf16[16,16,48]{2,0,1:T(8,128)(2,1)S(1)}, u32[]{:S(2)}, u32[]{:S(2)}) collective-permute-start(bf16[16,16,48]{2,0,1:T(8,128)(2,1)S(1)} %get-tuple-element.1351), channel_id=1, source_target_pairs={{15,0},{0,1},{1,2},{2,3},{3,4},{4,5},{5,6},{6,7},{7,8},{8,9},{9,10... | collective-permute-start | bytes 73736 | tf_op jit(solution)/shard_map/while/body/eval_jaxpr/ppermute | solution.py:23
  126.4 7.1 %collective-permute-start = (bf16[16,16,48]{2,0,1:T(8,128)(2,1)}, bf16[16,16,48]{2,0,1:T(8,128)(2,1)S(1)}, u32[]{:S(2)}, u32[]{:S(2)}) collective-permute-start(bf16[16,16,48]{2,0,1:T(8,128)(2,1)} %get-tuple-element.1350), channel_id=1, source_target_pairs={{15,0},{0,1},{1,2},{2,3},{3,4},{4,5},{5,6},{6,7},{7,8},{8,9},{9,10... | collective-permute-start | bytes 73736 | tf_op jit(solution)/shard_map/while/body/eval_jaxpr/ppermute | solution.py:23
  136.1 8.1 %collective-permute-start.1 = (bf16[16,16,48]{2,0,1:T(8,128)(2,1)S(1)}, bf16[16,16,48]{2,0,1:T(8,128)(2,1)S(1)}, u32[]{:S(2)}, u32[]{:S(2)}) collective-permute-start(bf16[16,16,48]{2,0,1:T(8,128)(2,1)S(1)} %get-tuple-element.1351), channel_id=1, source_target_pairs={{15,0},{0,1},{1,2},{2,3},{3,4},{4,5},{5,6},{6,7},{7,8},{8,9},{9,10... | collective-permute-start | bytes 73736 | tf_op jit(solution)/shard_map/while/body/eval_jaxpr/ppermute | solution.py:23
  136.2 7.1 %collective-permute-start = (bf16[16,16,48]{2,0,1:T(8,128)(2,1)}, bf16[16,16,48]{2,0,1:T(8,128)(2,1)S(1)}, u32[]{:S(2)}, u32[]{:S(2)}) collective-permute-start(bf16[16,16,48]{2,0,1:T(8,128)(2,1)} %get-tuple-element.1350), channel_id=1, source_target_pairs={{15,0},{0,1},{1,2},{2,3},{3,4},{4,5},{5,6},{6,7},{7,8},{8,9},{9,10... | collective-permute-start | bytes 73736 | tf_op jit(solution)/shard_map/while/body/eval_jaxpr/ppermute | solution.py:23
  146.0 8.1 %collective-permute-start.1 = (bf16[16,16,48]{2,0,1:T(8,128)(2,1)S(1)}, bf16[16,16,48]{2,0,1:T(8,128)(2,1)S(1)}, u32[]{:S(2)}, u32[]{:S(2)}) collective-permute-start(bf16[16,16,48]{2,0,1:T(8,128)(2,1)S(1)} %get-tuple-element.1351), channel_id=1, source_target_pairs={{15,0},{0,1},{1,2},{2,3},{3,4},{4,5},{5,6},{6,7},{7,8},{8,9},{9,10... | collective-permute-start | bytes 73736 | tf_op jit(solution)/shard_map/while/body/eval_jaxpr/ppermute | solution.py:23
  146.1 7.1 %collective-permute-start = (bf16[16,16,48]{2,0,1:T(8,128)(2,1)}, bf16[16,16,48]{2,0,1:T(8,128)(2,1)S(1)}, u32[]{:S(2)}, u32[]{:S(2)}) collective-permute-start(bf16[16,16,48]{2,0,1:T(8,128)(2,1)} %get-tuple-element.1350), channel_id=1, source_target_pairs={{15,0},{0,1},{1,2},{2,3},{3,4},{4,5},{5,6},{6,7},{7,8},{8,9},{9,10... | collective-permute-start | bytes 73736 | tf_op jit(solution)/shard_map/while/body/eval_jaxpr/ppermute | solution.py:23
  155.9 8.1 %collective-permute-start.1 = (bf16[16,16,48]{2,0,1:T(8,128)(2,1)S(1)}, bf16[16,16,48]{2,0,1:T(8,128)(2,1)S(1)}, u32[]{:S(2)}, u32[]{:S(2)}) collective-permute-start(bf16[16,16,48]{2,0,1:T(8,128)(2,1)S(1)} %get-tuple-element.1351), channel_id=1, source_target_pairs={{15,0},{0,1},{1,2},{2,3},{3,4},{4,5},{5,6},{6,7},{7,8},{8,9},{9,10... | collective-permute-start | bytes 73736 | tf_op jit(solution)/shard_map/while/body/eval_jaxpr/ppermute | solution.py:23
  155.9 7.1 %collective-permute-start = (bf16[16,16,48]{2,0,1:T(8,128)(2,1)}, bf16[16,16,48]{2,0,1:T(8,128)(2,1)S(1)}, u32[]{:S(2)}, u32[]{:S(2)}) collective-permute-start(bf16[16,16,48]{2,0,1:T(8,128)(2,1)} %get-tuple-element.1350), channel_id=1, source_target_pairs={{15,0},{0,1},{1,2},{2,3},{3,4},{4,5},{5,6},{6,7},{7,8},{8,9},{9,10... | collective-permute-start | bytes 73736 | tf_op jit(solution)/shard_map/while/body/eval_jaxpr/ppermute | solution.py:23
  165.7 8.1 %collective-permute-start.1 = (bf16[16,16,48]{2,0,1:T(8,128)(2,1)S(1)}, bf16[16,16,48]{2,0,1:T(8,128)(2,1)S(1)}, u32[]{:S(2)}, u32[]{:S(2)}) collective-permute-start(bf16[16,16,48]{2,0,1:T(8,128)(2,1)S(1)} %get-tuple-element.1351), channel_id=1, source_target_pairs={{15,0},{0,1},{1,2},{2,3},{3,4},{4,5},{5,6},{6,7},{7,8},{8,9},{9,10... | collective-permute-start | bytes 73736 | tf_op jit(solution)/shard_map/while/body/eval_jaxpr/ppermute | solution.py:23
  165.8 7.1 %collective-permute-start = (bf16[16,16,48]{2,0,1:T(8,128)(2,1)}, bf16[16,16,48]{2,0,1:T(8,128)(2,1)S(1)}, u32[]{:S(2)}, u32[]{:S(2)}) collective-permute-start(bf16[16,16,48]{2,0,1:T(8,128)(2,1)} %get-tuple-element.1350), channel_id=1, source_target_pairs={{15,0},{0,1},{1,2},{2,3},{3,4},{4,5},{5,6},{6,7},{7,8},{8,9},{9,10... | collective-permute-start | bytes 73736 | tf_op jit(solution)/shard_map/while/body/eval_jaxpr/ppermute | solution.py:23
  232.6 6.4 %collective-permute-start.2 = (bf16[16,16,48]{2,0,1:T(8,128)(2,1)S(1)}, bf16[16,16,48]{2,0,1:T(8,128)(2,1)S(1)}, u32[]{:S(2)}, u32[]{:S(2)}) collective-permute-start(bf16[16,16,48]{2,0,1:T(8,128)(2,1)S(1)} %fusion.235), channel_id=1, source_target_pairs={{15,0},{0,1},{1,2},{2,3},{3,4},{4,5},{5,6},{6,7},{7,8},{8,9},{9,10... | collective-permute-start | bytes 73736 | tf_op jit(solution)/shard_map/while/body/eval_jaxpr/ppermute | solution.py:23
  232.8 6.9 %collective-permute-start.3 = (bf16[16,16,48]{2,0,1:T(8,128)(2,1)S(1)}, bf16[16,16,48]{2,0,1:T(8,128)(2,1)S(1)}, u32[]{:S(2)}, u32[]{:S(2)}) collective-permute-start(bf16[16,16,48]{2,0,1:T(8,128)(2,1)S(1)} %fusion.236), channel_id=1, source_target_pairs={{15,0},{0,1},{1,2},{2,3},{3,4},{4,5},{5,6},{6,7},{7,8},{8,9},{9,10... | collective-permute-start | bytes 73736 | tf_op jit(solution)/shard_map/while/body/eval_jaxpr/ppermute | solution.py:23
  243.4 6.4 %collective-permute-start.2 = (bf16[16,16,48]{2,0,1:T(8,128)(2,1)S(1)}, bf16[16,16,48]{2,0,1:T(8,128)(2,1)S(1)}, u32[]{:S(2)}, u32[]{:S(2)}) collective-permute-start(bf16[16,16,48]{2,0,1:T(8,128)(2,1)S(1)} %fusion.235), channel_id=1, source_target_pairs={{15,0},{0,1},{1,2},{2,3},{3,4},{4,5},{5,6},{6,7},{7,8},{8,9},{9,10... | collective-permute-start | bytes 73736 | tf_op jit(solution)/shard_map/while/body/eval_jaxpr/ppermute | solution.py:23
  243.7 6.9 %collective-permute-start.3 = (bf16[16,16,48]{2,0,1:T(8,128)(2,1)S(1)}, bf16[16,16,48]{2,0,1:T(8,128)(2,1)S(1)}, u32[]{:S(2)}, u32[]{:S(2)}) collective-permute-start(bf16[16,16,48]{2,0,1:T(8,128)(2,1)S(1)} %fusion.236), channel_id=1, source_target_pairs={{15,0},{0,1},{1,2},{2,3},{3,4},{4,5},{5,6},{6,7},{7,8},{8,9},{9,10... | collective-permute-start | bytes 73736 | tf_op jit(solution)/shard_map/while/body/eval_jaxpr/ppermute | solution.py:23
  254.5 6.9 %collective-permute-start.3 = (bf16[16,16,48]{2,0,1:T(8,128)(2,1)S(1)}, bf16[16,16,48]{2,0,1:T(8,128)(2,1)S(1)}, u32[]{:S(2)}, u32[]{:S(2)}) collective-permute-start(bf16[16,16,48]{2,0,1:T(8,128)(2,1)S(1)} %fusion.236), channel_id=1, source_target_pairs={{15,0},{0,1},{1,2},{2,3},{3,4},{4,5},{5,6},{6,7},{7,8},{8,9},{9,10... | collective-permute-start | bytes 73736 | tf_op jit(solution)/shard_map/while/body/eval_jaxpr/ppermute | solution.py:23
  265.4 6.9 %collective-permute-start.3 = (bf16[16,16,48]{2,0,1:T(8,128)(2,1)S(1)}, bf16[16,16,48]{2,0,1:T(8,128)(2,1)S(1)}, u32[]{:S(2)}, u32[]{:S(2)}) collective-permute-start(bf16[16,16,48]{2,0,1:T(8,128)(2,1)S(1)} %fusion.236), channel_id=1, source_target_pairs={{15,0},{0,1},{1,2},{2,3},{3,4},{4,5},{5,6},{6,7},{7,8},{8,9},{9,10... | collective-permute-start | bytes 73736 | tf_op jit(solution)/shard_map/while/body/eval_jaxpr/ppermute | solution.py:23
  276.3 6.9 %collective-permute-start.3 = (bf16[16,16,48]{2,0,1:T(8,128)(2,1)S(1)}, bf16[16,16,48]{2,0,1:T(8,128)(2,1)S(1)}, u32[]{:S(2)}, u32[]{:S(2)}) collective-permute-start(bf16[16,16,48]{2,0,1:T(8,128)(2,1)S(1)} %fusion.236), channel_id=1, source_target_pairs={{15,0},{0,1},{1,2},{2,3},{3,4},{4,5},{5,6},{6,7},{7,8},{8,9},{9,10... | collective-permute-start | bytes 73736 | tf_op jit(solution)/shard_map/while/body/eval_jaxpr/ppermute | solution.py:23
  287.1 6.9 %collective-permute-start.3 = (bf16[16,16,48]{2,0,1:T(8,128)(2,1)S(1)}, bf16[16,16,48]{2,0,1:T(8,128)(2,1)S(1)}, u32[]{:S(2)}, u32[]{:S(2)}) collective-permute-start(bf16[16,16,48]{2,0,1:T(8,128)(2,1)S(1)} %fusion.236), channel_id=1, source_target_pairs={{15,0},{0,1},{1,2},{2,3},{3,4},{4,5},{5,6},{6,7},{7,8},{8,9},{9,10... | collective-permute-start | bytes 73736 | tf_op jit(solution)/shard_map/while/body/eval_jaxpr/ppermute | solution.py:23
  298.0 6.9 %collective-permute-start.3 = (bf16[16,16,48]{2,0,1:T(8,128)(2,1)S(1)}, bf16[16,16,48]{2,0,1:T(8,128)(2,1)S(1)}, u32[]{:S(2)}, u32[]{:S(2)}) collective-permute-start(bf16[16,16,48]{2,0,1:T(8,128)(2,1)S(1)} %fusion.236), channel_id=1, source_target_pairs={{15,0},{0,1},{1,2},{2,3},{3,4},{4,5},{5,6},{6,7},{7,8},{8,9},{9,10... | collective-permute-start | bytes 73736 | tf_op jit(solution)/shard_map/while/body/eval_jaxpr/ppermute | solution.py:23
  308.8 6.9 %collective-permute-start.3 = (bf16[16,16,48]{2,0,1:T(8,128)(2,1)S(1)}, bf16[16,16,48]{2,0,1:T(8,128)(2,1)S(1)}, u32[]{:S(2)}, u32[]{:S(2)}) collective-permute-start(bf16[16,16,48]{2,0,1:T(8,128)(2,1)S(1)} %fusion.236), channel_id=1, source_target_pairs={{15,0},{0,1},{1,2},{2,3},{3,4},{4,5},{5,6},{6,7},{7,8},{8,9},{9,10... | collective-permute-start | bytes 73736 | tf_op jit(solution)/shard_map/while/body/eval_jaxpr/ppermute | solution.py:23
  319.7 6.9 %collective-permute-start.3 = (bf16[16,16,48]{2,0,1:T(8,128)(2,1)S(1)}, bf16[16,16,48]{2,0,1:T(8,128)(2,1)S(1)}, u32[]{:S(2)}, u32[]{:S(2)}) collective-permute-start(bf16[16,16,48]{2,0,1:T(8,128)(2,1)S(1)} %fusion.236), channel_id=1, source_target_pairs={{15,0},{0,1},{1,2},{2,3},{3,4},{4,5},{5,6},{6,7},{7,8},{8,9},{9,10... | collective-permute-start | bytes 73736 | tf_op jit(solution)/shard_map/while/body/eval_jaxpr/ppermute | solution.py:23
  330.5 6.9 %collective-permute-start.3 = (bf16[16,16,48]{2,0,1:T(8,128)(2,1)S(1)}, bf16[16,16,48]{2,0,1:T(8,128)(2,1)S(1)}, u32[]{:S(2)}, u32[]{:S(2)}) collective-permute-start(bf16[16,16,48]{2,0,1:T(8,128)(2,1)S(1)} %fusion.236), channel_id=1, source_target_pairs={{15,0},{0,1},{1,2},{2,3},{3,4},{4,5},{5,6},{6,7},{7,8},{8,9},{9,10... | collective-permute-start | bytes 73736 | tf_op jit(solution)/shard_map/while/body/eval_jaxpr/ppermute | solution.py:23
  341.4 6.9 %collective-permute-start.3 = (bf16[16,16,48]{2,0,1:T(8,128)(2,1)S(1)}, bf16[16,16,48]{2,0,1:T(8,128)(2,1)S(1)}, u32[]{:S(2)}, u32[]{:S(2)}) collective-permute-start(bf16[16,16,48]{2,0,1:T(8,128)(2,1)S(1)} %fusion.236), channel_id=1, source_target_pairs={{15,0},{0,1},{1,2},{2,3},{3,4},{4,5},{5,6},{6,7},{7,8},{8,9},{9,10... | collective-permute-start | bytes 73736 | tf_op jit(solution)/shard_map/while/body/eval_jaxpr/ppermute | solution.py:23
  352.3 6.9 %collective-permute-start.3 = (bf16[16,16,48]{2,0,1:T(8,128)(2,1)S(1)}, bf16[16,16,48]{2,0,1:T(8,128)(2,1)S(1)}, u32[]{:S(2)}, u32[]{:S(2)}) collective-permute-start(bf16[16,16,48]{2,0,1:T(8,128)(2,1)S(1)} %fusion.236), channel_id=1, source_target_pairs={{15,0},{0,1},{1,2},{2,3},{3,4},{4,5},{5,6},{6,7},{7,8},{8,9},{9,10... | collective-permute-start | bytes 73736 | tf_op jit(solution)/shard_map/while/body/eval_jaxpr/ppermute | solution.py:23
  363.1 6.9 %collective-permute-start.3 = (bf16[16,16,48]{2,0,1:T(8,128)(2,1)S(1)}, bf16[16,16,48]{2,0,1:T(8,128)(2,1)S(1)}, u32[]{:S(2)}, u32[]{:S(2)}) collective-permute-start(bf16[16,16,48]{2,0,1:T(8,128)(2,1)S(1)} %fusion.236), channel_id=1, source_target_pairs={{15,0},{0,1},{1,2},{2,3},{3,4},{4,5},{5,6},{6,7},{7,8},{8,9},{9,10... | collective-permute-start | bytes 73736 | tf_op jit(solution)/shard_map/while/body/eval_jaxpr/ppermute | solution.py:23
  374.0 6.9 %collective-permute-start.3 = (bf16[16,16,48]{2,0,1:T(8,128)(2,1)S(1)}, bf16[16,16,48]{2,0,1:T(8,128)(2,1)S(1)}, u32[]{:S(2)}, u32[]{:S(2)}) collective-permute-start(bf16[16,16,48]{2,0,1:T(8,128)(2,1)S(1)} %fusion.236), channel_id=1, source_target_pairs={{15,0},{0,1},{1,2},{2,3},{3,4},{4,5},{5,6},{6,7},{7,8},{8,9},{9,10... | collective-permute-start | bytes 73736 | tf_op jit(solution)/shard_map/while/body/eval_jaxpr/ppermute | solution.py:23
  384.8 6.9 %collective-permute-start.3 = (bf16[16,16,48]{2,0,1:T(8,128)(2,1)S(1)}, bf16[16,16,48]{2,0,1:T(8,128)(2,1)S(1)}, u32[]{:S(2)}, u32[]{:S(2)}) collective-permute-start(bf16[16,16,48]{2,0,1:T(8,128)(2,1)S(1)} %fusion.236), channel_id=1, source_target_pairs={{15,0},{0,1},{1,2},{2,3},{3,4},{4,5},{5,6},{6,7},{7,8},{8,9},{9,10... | collective-permute-start | bytes 73736 | tf_op jit(solution)/shard_map/while/body/eval_jaxpr/ppermute | solution.py:23
  395.7 6.9 %collective-permute-start.3 = (bf16[16,16,48]{2,0,1:T(8,128)(2,1)S(1)}, bf16[16,16,48]{2,0,1:T(8,128)(2,1)S(1)}, u32[]{:S(2)}, u32[]{:S(2)}) collective-permute-start(bf16[16,16,48]{2,0,1:T(8,128)(2,1)S(1)} %fusion.236), channel_id=1, source_target_pairs={{15,0},{0,1},{1,2},{2,3},{3,4},{4,5},{5,6},{6,7},{7,8},{8,9},{9,10... | collective-permute-start | bytes 73736 | tf_op jit(solution)/shard_map/while/body/eval_jaxpr/ppermute | solution.py:23
  (71 other events, 465.4 us)
where the time goes:
time: 428 us; the launch traced here: 424 us
  waiting for transfers between devices  183 us (43%)
  local copies, waits for them, and re-layouts  82.2 us (19%)
  matrix products  80.5 us (19%)
  other arithmetic  65.6 us (15%)
  starting transfers between devices  6.55 us (2%)
    ppermute x62, waiting for transfers between devices, shifted(): return lax.ppermute(block, axis, route)  183 us
    and x31, other arithmetic, key_mask(): (key_pos < mask_count_total) & (sender_shards[None, :] // PARTS_IN_WINDOW...  22.5 us
    dot_general x16, matrix products, backward_update(): jnp.einsum('hab,bhe->ahe', logit_derivative, lookup_patch_group, preferre...  17.1 us
    dot_general x16, matrix products, backward_update(): jnp.einsum('nij,bij->inb', thinned_probes, lookup_patch_group, preferred_...  16 us
    dot_general x16, matrix products, backward_update(): jnp.einsum('nij,bij->inb', sparse_output_gradient, value_tile_block, pref...  16 us
    unnamed x122, local copies, waits for them, and re-layouts  14.1 us
    and x16, other arithmetic, backward_update(): allowed & query_mask  11.5 us
    while x45, local copies, waits for them, and re-layouts  9.6 us
  transfers between devices with their start and end apart: 62, of which 47 were waited for; matrix products, arithmetic and copies ran while one was open for 11% of the time, Pallas kernels for 0%

commit v1 on v0

v1 whole, which is shorter than its diff:
```python
import math

import jax
import jax.numpy as jnp
from jax import lax
from jax.experimental import pallas as pl
from jax.experimental.pallas import tpu as pltpu
from jax.sharding import PartitionSpec as P

STEP = 16
WINDOW = 16
FLOOR = -1e30
LOG2E = 1.4426950408889634
EARLY_HEADS = 6

BF = jnp.bfloat16
F32 = jnp.float32


def nn(a, b):
    return lax.dot_general(a, b, (((1,), (0,)), ((), ())), preferred_element_type=F32)


def nt(a, b):
    return lax.dot_general(a, b, (((1,), (1,)), ((), ())), preferred_element_type=F32)


def tn(a, b):
    return lax.dot_general(a, b, (((0,), (0,)), ((), ())), preferred_element_type=F32)


def parts_of(x, count):
    out = []
    for _ in range(count - 1):
        head = x.astype(BF).astype(F32)
        out.append(head)
        x = x - head
    out.append(x)
    return out


def rows_block(rows, height, width):
    at = lax.broadcasted_iota(jnp.int32, (height, width), 0)
    block = jnp.zeros((height, width), F32)
    for n, row in enumerate(rows):
        block = jnp.where(at == n, row, block)
    return block


def kernel(
    span_ref, res_ref, count_ref, q_ref, k_ref, v_ref, g_ref,
    dq_ref, dk_ref, dv_ref,
    qt, kt, vt, gt, dqt, dkt, dvt, qb, gb, pick, far, pb, dpb,
    send1, recv1, send2, recv2, ss1, rs1, ss2, rs2,
):
    tokens, width = q_ref.shape
    heads = span_ref.shape[0]
    dim = width // heads
    few = tokens // STEP
    chosen = heads * few
    scale = 1.0 / math.sqrt(dim)
    scale2 = scale * LOG2E
    me = lax.axis_index("seq")
    base = (me // WINDOW) * WINDOW
    my = me - base
    count = count_ref[0]

    def partner(n):
        return lax.rem(my + n, WINDOW)

    barrier = pltpu.get_barrier_semaphore()

    def greet(n, carry):
        pl.semaphore_signal(
            barrier, inc=1, device_id={"seq": base + partner(n)},
            device_id_type=pl.DeviceIdType.MESH,
        )
        return carry

    lax.fori_loop(1, WINDOW, greet, 0)

    def block_of(n):
        return pl.ds(pl.multiple_of(n * few, few), few)

    def exchange(n, source, target, send_sem, recv_sem):
        to = partner(n)
        return pltpu.make_async_remote_copy(
            src_ref=source.at[block_of(to)],
            dst_ref=target.at[block_of(my)],
            send_sem=send_sem.at[n],
            recv_sem=recv_sem.at[n],
            device_id={"seq": base + to},
            device_id_type=pl.DeviceIdType.MESH,
        )

    def start_all(*args):
        def step(n, carry):
            exchange(n, *args).start()
            return carry

        lax.fori_loop(1, WINDOW, step, 0)

    def wait_all(*args):
        def step(n, carry):
            exchange(n, *args).wait()
            return carry

        lax.fori_loop(1, WINDOW, step, 0)

    lane = lax.broadcasted_iota(jnp.int32, (1, chosen), 1)
    lane_head = lane // few
    lane_res = jnp.zeros((1, chosen), jnp.int32)
    lane_span = jnp.zeros((1, chosen), jnp.int32)
    for h in range(heads):
        lane_res = jnp.where(lane_head == h, res_ref[h], lane_res)
        lane_span = jnp.where(lane_head == h, span_ref[h], lane_span)
    lane_token = (lane % few) * STEP + lane_res
    row = lax.broadcasted_iota(jnp.int32, (tokens, tokens), 0)
    col = lax.broadcasted_iota(jnp.int32, (tokens, tokens), 1)
    start = me * tokens
    huge = jnp.int32(1 << 20)
    row_ok = row + start < count
    far[...] = jnp.where(row_ok, row ^ col, huge)
    pick[...] = (row == lane_token).astype(F32).astype(BF)

    qt[...] = q_ref[...].T
    kt[...] = k_ref[...].T
    vt[...] = v_ref[...].T
    gt[...] = g_ref[...].T

    def picked(source, keep):
        full = nn(source[...], pick[...])
        total = jnp.zeros((dim, chosen), F32)
        for h in range(heads):
            part = jnp.where(lane_head == h, full[h * dim : (h + 1) * dim], 0.0)
            if keep is not None:
                keep[h * dim : (h + 1) * dim, :] = part.astype(BF)
            total = total + part
        return total

    q_few = picked(qt, qb)
    g_few = picked(gt, gb)
    k_few = picked(kt, None)
    v_few = picked(vt, None)

    mask = jnp.where(row_ok, row ^ lane_token, huge) < lane_span
    s = jnp.where(mask, nn(k_ref[...], qb[...]) * scale2, FLOOR)
    top = jnp.max(s, axis=0, keepdims=True)
    p = jnp.exp2(s - top)
    total = jnp.sum(p, axis=0, keepdims=True)
    p = p * (1.0 / total)
    dp = nn(v_ref[...], gb[...])
    local_lse = top + jnp.log(total) * LOG2E
    local_delta = jnp.sum(p * dp, axis=0, keepdims=True)
    pb[...] = p
    dpb[...] = dp
    tail = chosen - 4 * dim
    stats = rows_block(parts_of(local_lse, 3) + parts_of(local_delta, 2), tail, chosen)
    packed = jnp.concatenate([q_few, k_few, v_few, g_few, stats], axis=0)
    send1[...] = packed.T.astype(BF)

    pl.semaphore_wait(barrier, WINDOW - 1)
    start_all(send1, recv1, ss1, rs1)
    recv1[block_of(my), :] = send1[block_of(my), :]

    query_ok = lane + start < count

    def local_head(h, carry):
        at = pl.ds(pl.multiple_of(h * dim, 16), dim)
        qh, kh, vh, gh = qt[at, :], kt[at, :], vt[at, :], gt[at, :]
        s = jnp.where(far[...] < span_ref[h], tn(kh, qh) * scale2, FLOOR)
        top = jnp.max(s, axis=0, keepdims=True)
        p = jnp.exp2(s - top)
        inverse = 1.0 / jnp.sum(p, axis=0, keepdims=True)
        dp = tn(vh, gh)
        delta = jnp.sum(p * dp, axis=0, keepdims=True) * inverse
        keep = query_ok & (lane % STEP != res_ref[h])
        w = p * jnp.where(keep, inverse, 0.0)
        ds = (w * (dp - delta)).astype(BF)
        dqt[at, :] = nn(kh, ds) * scale
        dkt[at, :] = nt(qh, ds) * scale
        dvt[at, :] = nt(gh, w.astype(BF))
        return carry

    lax.fori_loop(0, EARLY_HEADS, local_head, 0)

    wait_all(send1, recv1, ss1, rs1)
    got = recv1[...].astype(F32).T
    got_half = got.astype(BF)
    qh, kh = got_half[0:dim], got_half[dim : 2 * dim]
    vh, gh = got_half[2 * dim : 3 * dim], got_half[3 * dim : 4 * dim]
    at = 4 * dim
    local_lse = got[at : at + 1] + got[at + 1 : at + 2] + got[at + 2 : at + 3]
    local_delta = got[at + 3 : at + 4] + got[at + 4 : at + 5]
    limit = count - base * tokens - res_ref[my]
    s = jnp.where(row * STEP < limit, tn(kh, qh) * scale2, FLOOR)
    top = jnp.max(s, axis=0, keepdims=True)
    p = jnp.exp2(s - top)
    total = jnp.sum(p, axis=0, keepdims=True)
    dilated_lse = top + jnp.log(total) * LOG2E
    most = jnp.maximum(local_lse, dilated_lse)
    both = most + jnp.log(jnp.exp2(local_lse - most) + jnp.exp2(dilated_lse - most)) * LOG2E
    here_ok = lane * STEP < limit
    local_part = jnp.where(here_ok, jnp.exp2(local_lse - both), 0.0)
    u = p * jnp.where(here_ok, jnp.exp2(top - both), 0.0)
    dp = tn(vh, gh)
    delta = local_part * local_delta + jnp.sum(u * dp, axis=0, keepdims=True)
    delta = jnp.where(here_ok, delta, 0.0)
    ds = (u * (dp - delta)).astype(BF)
    stats = rows_block(parts_of(local_part, 2) + parts_of(delta, 2), chosen - 3 * dim, chosen)
    packed = jnp.concatenate(
        [nn(kh, ds) * scale, nt(qh, ds) * scale, nt(gh, u.astype(BF)), stats], axis=0
    )
    send2[...] = packed.T.astype(BF)
    start_all(send2, recv2, ss2, rs2)
    recv2[block_of(my), :] = send2[block_of(my), :]

    lax.fori_loop(EARLY_HEADS, heads, local_head, 0)

    wait_all(send2, recv2, ss2, rs2)
    back = recv2[...].astype(F32).T
    at = 3 * dim
    local_part = back[at : at + 1] + back[at + 1 : at + 2]
    delta = back[at + 2 : at + 3] + back[at + 3 : at + 4]
    w = pb[...] * local_part
    ds = (w * (dpb[...] - delta)).astype(BF)
    wide = nn(kt[...], ds) * scale
    dq_few, dk_few, dv_few = back[0:dim], back[dim : 2 * dim], back[2 * dim : 3 * dim]

    def spread(piece_of):
        pieces = [
            jnp.where(lane_head == h, piece_of(h), 0.0).astype(BF) for h in range(heads)
        ]
        return nt(jnp.concatenate(pieces, axis=0), pick[...])

    dq = dqt[...] + spread(lambda h: wide[h * dim : (h + 1) * dim] + dq_few)
    dq_ref[...] = dq.T.astype(BF)
    dk = dkt[...] + nt(qb[...], ds) * scale + spread(lambda h: dk_few)
    dk_ref[...] = dk.T.astype(BF)
    dv = dvt[...] + nt(gb[...], w.astype(BF)) + spread(lambda h: dv_few)
    dv_ref[...] = dv.T.astype(BF)


def shards(queries, keys, values, grad_out, local_span, head_residue, valid_count):
    tokens, width = queries.shape
    heads = local_span.shape[0]
    chosen = heads * (tokens // STEP)
    assert heads == WINDOW and chosen == tokens
    smem = pl.BlockSpec(memory_space=pltpu.SMEM)
    vmem = pl.BlockSpec(memory_space=pltpu.VMEM)
    out = jax.ShapeDtypeStruct((tokens, width), BF)
    return pl.pallas_call(
        kernel,
        out_shape=(out, out, out),
        in_specs=[smem] * 3 + [vmem] * 4,
        out_specs=(vmem, vmem, vmem),
        scratch_shapes=[pltpu.VMEM((width, tokens), BF)] * 4
        + [pltpu.VMEM((width, tokens), F32)] * 3
        + [pltpu.VMEM((width, chosen), BF)] * 2
        + [
            pltpu.VMEM((tokens, chosen), BF),
            pltpu.VMEM((tokens, tokens), jnp.int32),
            pltpu.VMEM((tokens, chosen), F32),
            pltpu.VMEM((tokens, chosen), F32),
        ]
        + [pltpu.VMEM((chosen, chosen), BF)] * 4
        + [pltpu.SemaphoreType.DMA((WINDOW,))] * 4,
        compiler_params=pltpu.CompilerParams(
            collective_id=0, has_side_effects=True, vmem_limit_bytes=40 * 2**20
        ),
    )(local_span, head_residue, valid_count, queries, keys, values, grad_out)


def solution(mesh):
    rows = P(("groups", "seq"), None)
    return jax.shard_map(
        shards,
        mesh=mesh,
        in_specs=(rows, rows, rows, rows, P(), P(), P("groups")),
        out_specs=(rows, rows, rows),
        check_vma=False,
    )
```

time: 428 us -> 26.4 us (0.06)
  waiting for transfers between devices: 183 us -> 0 us
  matrix products: 80.5 us -> 0 us
  local copies, waits for them, and re-layouts: 82.2 us -> 6.22 us
  other arithmetic: 65.6 us -> 0 us
  Pallas kernels: 0 us -> 18.6 us
  starting transfers between devices: 6.55 us -> 0 us
    ppermute x62 -> x0, waiting for transfers between devices: 183 us -> none  [shifted(): return lax.ppermute(block, axis, route)]
    dot_general x141 -> x0, matrix products: 80.5 us -> none  [the longest x16 17.1 us: backward_update(): jnp.einsum('hab,bhe->ahe', logit_derivative, lookup_patch_group, preferre...]
    and x47 -> x0, other arithmetic: 34 us -> none  [the longest x31 22.5 us: key_mask(): (key_pos < mask_count_total) & (sender_shards[None, :] // PARTS_IN_WINDOW...]
    dynamic_update_slice x30 -> x0, local copies, waits for them, and re-layouts: 19 us -> none  [the longest x15 9.56 us: forward_hop_step(): lax.dynamic_update_index_in_dim(kept_values, blocks[1], hop_index, 0)]
    pallas_call x0 -> x1, Pallas kernels: none -> 18.6 us  [shards(): pl.pallas_call(kernel, out_shape=(out, out, out), in_specs=[smem] * 3 + [...]
    reshape x5 -> x0, local copies, waits for them, and re-layouts: 11.1 us -> none  [the longest x3 8 us: distribute_heads(): return full_rows.reshape(-1, picked.shape[1], picked.shape[2])]
    while x50 -> x0, local copies, waits for them, and re-layouts: 11.1 us -> none
    convert_element_type x39 -> x0, other arithmetic: 10.2 us -> none  [the longest x1 3.47 us: shards(): weight_half = weight.astype(jnp.bfloat16)]
  transfers between devices with their start and end apart: 62 -> 0, of which waited for: 47 -> 0; matrix products, arithmetic and copies ran while one was open for 11% -> 0% of each run, Pallas kernels for 0% -> 0%
where the time goes in v1:
time: 26.4 us; the launch traced here: 26.2 us
  Pallas kernels  18.6 us (70%)
  local copies, waits for them, and re-layouts  6.22 us (24%)
  between operations  1.35 us (5%)
    pallas_call x1, Pallas kernels, shards(): pl.pallas_call(kernel, out_shape=(out, out, out), in_specs=[smem] * 3 + [...  18.6 us
    unnamed x15, local copies, waits for them, and re-layouts  6.22 us

profile of v1, /device:TPU:0, one launch (start us, length us, event | category | flops | bytes accessed | tf_op | source)
XLA Modules:
  0.0 26.2 jit_solution(6532590727216744664)
XLA Ops:
  0.6 0.0 copy-start.5
  0.6 0.0 copy-start.4
  1.3 0.0 copy-done.5
  1.3 0.0 copy-done.4
  1.3 0.0 copy-start
  1.3 1.0 %copy-done = bf16[256,768]{1,0:T(8,128)(2,1)S(1)} copy-done((bf16[256,768]{1,0:T(8,128)(2,1)S(1)}, bf16[256,768]{1,0:T(8,128)(2,1)}, u32[]{:S(2)}) %copy-start) | copy-done | bytes 393240
  2.3 0.0 copy-start.1
  2.3 1.0 %copy-done.1 = bf16[256,768]{1,0:T(8,128)(2,1)S(1)} copy-done((bf16[256,768]{1,0:T(8,128)(2,1)S(1)}, bf16[256,768]{1,0:T(8,128)(2,1)}, u32[]{:S(2)}) %copy-start.1) | copy-done | bytes 393240
  3.3 0.0 copy-start.2
  3.3 1.0 %copy-done.2 = bf16[256,768]{1,0:T(8,128)(2,1)S(1)} copy-done((bf16[256,768]{1,0:T(8,128)(2,1)S(1)}, bf16[256,768]{1,0:T(8,128)(2,1)}, u32[]{:S(2)}) %copy-start.2) | copy-done | bytes 393240
  4.3 0.0 copy-start.3
  4.3 1.0 %copy-done.3 = bf16[256,768]{1,0:T(8,128)(2,1)S(1)} copy-done((bf16[256,768]{1,0:T(8,128)(2,1)S(1)}, bf16[256,768]{1,0:T(8,128)(2,1)}, u32[]{:S(2)}) %copy-start.3) | copy-done | bytes 393240
  5.3 18.6 %shard_map.94 = (bf16[256,768]{1,0:T(8,128)(2,1)S(1)}, bf16[256,768]{1,0:T(8,128)(2,1)S(1)}, bf16[256,768]{1,0:T(8,128)(2,1)S(1)}) custom-call(s32[16]{0:T(128)S(1)} %copy-done.4, s32[16]{0:T(128)S(1)} %copy-done.5, s32[1]{0:T(128)S(6)} %copy.13.count_ref, bf16[256,768]{1,0:T(8,128)(2,1)S(1)} %copy-done, bf16[256,768]{1,0:T(8,128)(2,1)S(1)} %copy-done.1, ...), custom_call_target="tpu_custom_call" | custom-call | tf_op jit(solution)/shard_map/pallas_call | solution.py:252
  23.9 0.7 %copy.14 = bf16[256,768]{1,0:T(8,128)(2,1)} copy(bf16[256,768]{1,0:T(8,128)(2,1)S(1)} %get-tuple-element.6) | data formatting | bytes 786432
  24.7 0.7 %copy.15 = bf16[256,768]{1,0:T(8,128)(2,1)} copy(bf16[256,768]{1,0:T(8,128)(2,1)S(1)} %get-tuple-element.7) | data formatting | bytes 786432
  25.4 0.7 %copy.16 = bf16[256,768]{1,0:T(8,128)(2,1)} copy(bf16[256,768]{1,0:T(8,128)(2,1)S(1)} %get-tuple-element.8) | data formatting | bytes 786432
Async XLA Ops:
  0.6 0.7 %copy-start.5 = (s32[16]{0:T(128)S(1)}, s32[16]{0:T(128)}, u32[]{:S(2)}) copy-start(s32[16]{0:T(128)} %res_ref.1) | copy-start | bytes 196
  0.6 0.7 %copy-start.4 = (s32[16]{0:T(128)S(1)}, s32[16]{0:T(128)}, u32[]{:S(2)}) copy-start(s32[16]{0:T(128)} %span_ref.1) | copy-start | bytes 196
  1.3 1.0 %copy-start = (bf16[256,768]{1,0:T(8,128)(2,1)S(1)}, bf16[256,768]{1,0:T(8,128)(2,1)}, u32[]{:S(2)}) copy-start(bf16[256,768]{1,0:T(8,128)(2,1)} %q_ref.1) | copy-start | bytes 1179652
  2.3 1.0 %copy-start.1 = (bf16[256,768]{1,0:T(8,128)(2,1)S(1)}, bf16[256,768]{1,0:T(8,128)(2,1)}, u32[]{:S(2)}) copy-start(bf16[256,768]{1,0:T(8,128)(2,1)} %k_ref.1) | copy-start | bytes 1179652
  3.3 1.0 %copy-start.2 = (bf16[256,768]{1,0:T(8,128)(2,1)S(1)}, bf16[256,768]{1,0:T(8,128)(2,1)}, u32[]{:S(2)}) copy-start(bf16[256,768]{1,0:T(8,128)(2,1)} %v_ref.1) | copy-start | bytes 1179652
  4.3 1.0 %copy-start.3 = (bf16[256,768]{1,0:T(8,128)(2,1)S(1)}, bf16[256,768]{1,0:T(8,128)(2,1)}, u32[]{:S(2)}) copy-start(bf16[256,768]{1,0:T(8,128)(2,1)} %g_ref.1) | copy-start | bytes 1179652

commit v2 on v1

--- a/solution.py
+++ b/solution.py
@@ -12,6 +12,7 @@
 FLOOR = -1e30
 LOG2E = 1.4426950408889634
 EARLY_HEADS = 6
+VMEM_LIMIT = 63 * 2**20
 
 BF = jnp.bfloat16
 F32 = jnp.float32
@@ -48,9 +49,9 @@
 
 
 def kernel(
-    span_ref, res_ref, count_ref, q_ref, k_ref, v_ref, g_ref,
-    dq_ref, dk_ref, dv_ref,
-    qt, kt, vt, gt, dqt, dkt, dvt, qb, gb, pick, far, pb, dpb,
+    span_ref, res_ref, count_ref, q_hbm, k_hbm, v_hbm, g_hbm,
+    dq_hbm, dk_hbm, dv_hbm,
+    dq_ref, dk_ref, dv_ref, store_sem, q_ref, k_ref, v_ref, g_ref, load_sem, qt, kt, vt, gt, dqt, dkt, dvt, qb, gb, pick, far, pb, dpb,
     send1, recv1, send2, recv2, ss1, rs1, ss2, rs2,
 ):
     tokens, width = q_ref.shape
@@ -64,6 +65,14 @@
     base = (me // WINDOW) * WINDOW
     my = me - base
     count = count_ref[0]
+    loads = [
+        pltpu.make_async_copy(source, target, load_sem.at[n])
+        for n, (source, target) in enumerate(
+            ((q_hbm, q_ref), (g_hbm, g_ref), (k_hbm, k_ref), (v_hbm, v_ref))
+        )
+    ]
+    for load in loads:
+        load.start()
 
     def partner(n):
         return lax.rem(my + n, WINDOW)
@@ -123,10 +132,11 @@
     far[...] = jnp.where(row_ok, row ^ col, huge)
     pick[...] = (row == lane_token).astype(F32).astype(BF)
 
-    qt[...] = q_ref[...].T
-    kt[...] = k_ref[...].T
-    vt[...] = v_ref[...].T
-    gt[...] = g_ref[...].T
+    for load, source, target in zip(
+        loads, (q_ref, g_ref, k_ref, v_ref), (qt, gt, kt, vt)
+    ):
+        load.wait()
+        target[...] = source[...].T
 
     def picked(source, keep):
         full = nn(source[...], pick[...])
@@ -182,7 +192,7 @@
         dvt[at, :] = nt(gh, w.astype(BF))
         return carry
 
-    lax.fori_loop(0, EARLY_HEADS, local_head, 0)
+    lax.fori_loop(0, EARLY_HEADS, local_head, 0, unroll=2)
 
     wait_all(send1, recv1, ss1, rs1)
     got = recv1[...].astype(F32).T
@@ -215,7 +225,7 @@
     start_all(send2, recv2, ss2, rs2)
     recv2[block_of(my), :] = send2[block_of(my), :]
 
-    lax.fori_loop(EARLY_HEADS, heads, local_head, 0)
+    lax.fori_loop(EARLY_HEADS, heads, local_head, 0, unroll=2)
 
     wait_all(send2, recv2, ss2, rs2)
     back = recv2[...].astype(F32).T
@@ -233,12 +243,42 @@
         ]
         return nt(jnp.concatenate(pieces, axis=0), pick[...])
 
+    def store(n, source, target):
+        copy = pltpu.make_async_copy(source, target, store_sem.at[n])
+        copy.start()
+        return copy
+
     dq = dqt[...] + spread(lambda h: wide[h * dim : (h + 1) * dim] + dq_few)
-    dq_ref[...] = dq.T.astype(BF)
+    dq_ref[...] = dq.astype(BF)
+    store_dq = store(0, dq_ref, dq_hbm)
     dk = dkt[...] + nt(qb[...], ds) * scale + spread(lambda h: dk_few)
-    dk_ref[...] = dk.T.astype(BF)
+    dk_ref[...] = dk.astype(BF)
+    store_dk = store(1, dk_ref, dk_hbm)
     dv = dvt[...] + nt(gb[...], w.astype(BF)) + spread(lambda h: dv_few)
-    dv_ref[...] = dv.T.astype(BF)
+    dv_ref[...] = dv.astype(BF)
+    store_dv = store(2, dv_ref, dv_hbm)
+    store_dq.wait()
+    store_dk.wait()
+    store_dv.wait()
+
+
+def finish(a_in, b_in, c_in, a_out, b_out, c_out, sources, targets, load_sem, store_sem):
+    loads = [
+        pltpu.make_async_copy(ref, sources.at[n], load_sem.at[n])
+        for n, ref in enumerate((a_in, b_in, c_in))
+    ]
+    for load in loads:
+        load.start()
+    stores = [
+        pltpu.make_async_copy(targets.at[n], ref, store_sem.at[n])
+        for n, ref in enumerate((a_out, b_out, c_out))
+    ]
+    for n in range(3):
+        loads[n].wait()
+        targets[n] = sources[n].T
+        stores[n].start()
+    for store in stores:
+        store.wait()
 
 
 def shards(queries, keys, values, grad_out, local_span, head_residue, valid_count):
@@ -248,13 +288,19 @@
     assert heads == WINDOW and chosen == tokens
     smem = pl.BlockSpec(memory_space=pltpu.SMEM)
     vmem = pl.BlockSpec(memory_space=pltpu.VMEM)
+    hbm = pl.BlockSpec(memory_space=pltpu.MemorySpace.HBM)
     out = jax.ShapeDtypeStruct((tokens, width), BF)
-    return pl.pallas_call(
+    turned = jax.ShapeDtypeStruct((width, tokens), BF)
+    gradients = pl.pallas_call(
         kernel,
-        out_shape=(out, out, out),
-        in_specs=[smem] * 3 + [vmem] * 4,
-        out_specs=(vmem, vmem, vmem),
-        scratch_shapes=[pltpu.VMEM((width, tokens), BF)] * 4
+        out_shape=(turned, turned, turned),
+        in_specs=[smem] * 3 + [hbm] * 4,
+        out_specs=(hbm, hbm, hbm),
+        scratch_shapes=[pltpu.VMEM((width, tokens), BF)] * 3
+        + [pltpu.SemaphoreType.DMA((3,))]
+        + [pltpu.VMEM((tokens, width), BF)] * 4
+        + [pltpu.SemaphoreType.DMA((4,))]
+        + [pltpu.VMEM((width, tokens), BF)] * 4
         + [pltpu.VMEM((width, tokens), F32)] * 3
         + [pltpu.VMEM((width, chosen), BF)] * 2
         + [
@@ -266,9 +312,22 @@
         + [pltpu.VMEM((chosen, chosen), BF)] * 4
         + [pltpu.SemaphoreType.DMA((WINDOW,))] * 4,
         compiler_params=pltpu.CompilerParams(
-            collective_id=0, has_side_effects=True, vmem_limit_bytes=40 * 2**20
+            collective_id=0, has_side_effects=True, vmem_limit_bytes=VMEM_LIMIT
         ),
     )(local_span, head_residue, valid_count, queries, keys, values, grad_out)
+    return pl.pallas_call(
+        finish,
+        out_shape=(out, out, out),
+        in_specs=[hbm] * 3,
+        out_specs=(hbm, hbm, hbm),
+        scratch_shapes=[
+            pltpu.VMEM((3, width, tokens), BF),
+            pltpu.VMEM((3, tokens, width), BF),
+            pltpu.SemaphoreType.DMA((3,)),
+            pltpu.SemaphoreType.DMA((3,)),
+        ],
+        compiler_params=pltpu.CompilerParams(vmem_limit_bytes=VMEM_LIMIT),
+    )(*gradients)
 
 
 def solution(mesh):

time: 26.4 us -> 23.2 us (0.88)
  local copies, waits for them, and re-layouts: 6.22 us -> 0 us
  Pallas kernels: 18.6 us -> 21.7 us
    unnamed x15 -> x0, local copies, waits for them, and re-layouts: 6.22 us -> none
    pallas_call x1 -> x2, Pallas kernels: 18.6 us -> 21.7 us  [the longest x1 19.5 us: shards(): pl.pallas_call(kernel, out_shape=(turned, turned, turned), in_specs=[smem...]
where the time goes in v2:
time: 23.2 us; the launch traced here: 23 us
  Pallas kernels  21.7 us (94%)
  between operations  1.29 us (6%)
    pallas_call x1, Pallas kernels, shards(): pl.pallas_call(kernel, out_shape=(turned, turned, turned), in_specs=[smem...  19.5 us
    pallas_call x1, Pallas kernels, shards(): pl.pallas_call(finish, out_shape=(out, out, out), in_specs=[hbm] * 3, out...  2.26 us

profile of v2, /device:TPU:0, one launch (start us, length us, event | category | flops | bytes accessed | tf_op | source)
XLA Modules:
  0.0 23.0 jit_solution(11563023890668047762)
XLA Ops:
  1.3 19.5 %shard_map.94 = (bf16[768,256]{1,0:T(8,128)(2,1)}, bf16[768,256]{1,0:T(8,128)(2,1)}, bf16[768,256]{1,0:T(8,128)(2,1)}) custom-call(s32[16]{0:T(128)} %span_ref.1, s32[16]{0:T(128)} %res_ref.1, s32[1]{0:T(128)S(6)} %copy.10.count_ref, bf16[256,768]{1,0:T(8,128)(2,1)} %q_hbm.1, bf16[256,768]{1,0:T(8,128)(2,1)} %k_hbm.1, bf16[256,768]{1,0:T(8,128)(2,1)} %v_hbm.1, ...), custom_call_target="tpu_custom_call" | custom-call | tf_op jit(solution)/shard_map/pallas_call | solution.py:294
  20.7 2.3 %shard_map.95 = (bf16[256,768]{1,0:T(8,128)(2,1)}, bf16[256,768]{1,0:T(8,128)(2,1)}, bf16[256,768]{1,0:T(8,128)(2,1)}) custom-call(bf16[768,256]{1,0:T(8,128)(2,1)} %get-tuple-element.6.a_in, bf16[768,256]{1,0:T(8,128)(2,1)} %get-tuple-element.7.b_in, bf16[768,256]{1,0:T(8,128)(2,1)} %get-tuple-element.8.c_in), custom_call_target="tpu_custom_call" | custom-call | tf_op jit(solution)/shard_map/pallas_call | solution.py:318

commit v3 on v1

v3 whole, which is shorter than its diff:
```python
import math

import jax
import jax.numpy as jnp
from jax import lax
from jax.experimental import pallas as pl
from jax.experimental.pallas import tpu as pltpu
from jax.sharding import PartitionSpec as P

STEP = 16
WINDOW = 16
FLOOR = -1e30
LOG2E = 1.4426950408889634
EARLY_HEADS = 6
VMEM_LIMIT = 63 * 2**20

BF = jnp.bfloat16
F32 = jnp.float32


def nn(a, b):
    return lax.dot_general(a, b, (((1,), (0,)), ((), ())), preferred_element_type=F32)


def nt(a, b):
    return lax.dot_general(a, b, (((1,), (1,)), ((), ())), preferred_element_type=F32)


def tn(a, b):
    return lax.dot_general(a, b, (((0,), (0,)), ((), ())), preferred_element_type=F32)


def parts_of(x, count):
    out = []
    for _ in range(count - 1):
        head = x.astype(BF).astype(F32)
        out.append(head)
        x = x - head
    out.append(x)
    return out


def rows_block(rows, height, width):
    at = lax.broadcasted_iota(jnp.int32, (height, width), 0)
    block = jnp.zeros((height, width), F32)
    for n, row in enumerate(rows):
        block = jnp.where(at == n, row, block)
    return block


def one_hot(condition):
    return condition.astype(F32).astype(BF)


def fold_matrix(heads, dim, wide, offset):
    feature = lax.broadcasted_iota(jnp.int32, (dim, wide), 1)
    column = lax.broadcasted_iota(jnp.int32, (dim, wide), 0)
    return jnp.concatenate([one_hot(feature == column + offset)] * heads, axis=0)


def stat_matrix(wide, offset):
    feature = lax.broadcasted_iota(jnp.int32, (16, wide), 1)
    return one_hot(feature == lax.broadcasted_iota(jnp.int32, (16, wide), 0) + offset)


def lane_tokens(res_ref, chosen, few):
    lane = lax.broadcasted_iota(jnp.int32, (1, chosen), 1)
    residue = jnp.zeros((1, chosen), jnp.int32)
    for h in range(chosen // few):
        residue = jnp.where(lane // few == h, res_ref[h], residue)
    return (lane % few) * STEP + residue


def own_columns(chosen, width, few, dim):
    row = lax.broadcasted_iota(jnp.int32, (chosen, 1), 0)
    column = lax.broadcasted_iota(jnp.int32, (1, width), 1)
    return (row // few) == (column // dim)


def kernel(
    span_ref, res_ref, count_ref, q_hbm, k_hbm, v_hbm, g_hbm,
    recv2, pb_hbm, dpb_hbm, qb_hbm, gb_hbm, dq_hbm, dk_hbm, dv_hbm,
    q_ref, k_ref, v_ref, g_ref, load_sem, store_sem, own_sem,
    qt, kt, vt, gt, dqt, dkt, dvt, dq_ref, dk_ref, dv_ref, qb, gb, far, pb, dpb,
    send1, recv1, send2, ss1, rs1, ss2, rs2,
):
    tokens, width = q_ref.shape
    heads = span_ref.shape[0]
    dim = width // heads
    few = tokens // STEP
    chosen = heads * few
    scale = 1.0 / math.sqrt(dim)
    scale2 = scale * LOG2E
    me = lax.axis_index("seq")
    base = (me // WINDOW) * WINDOW
    my = me - base
    count = count_ref[0]
    loads = [
        pltpu.make_async_copy(source, target, load_sem.at[n])
        for n, (source, target) in enumerate(
            ((q_hbm, q_ref), (g_hbm, g_ref), (k_hbm, k_ref), (v_hbm, v_ref))
        )
    ]
    for load in loads:
        load.start()

    def partner(n):
        return lax.rem(my + n, WINDOW)

    barrier = pltpu.get_barrier_semaphore()

    def greet(n, carry):
        pl.semaphore_signal(
            barrier, inc=1, device_id={"seq": base + partner(n)},
            device_id_type=pl.DeviceIdType.MESH,
        )
        return carry

    lax.fori_loop(1, WINDOW, greet, 0)

    def block_of(n):
        return pl.ds(pl.multiple_of(n * few, few), few)

    def exchange(n, source, target, send_sem, recv_sem):
        to = partner(n)
        return pltpu.make_async_remote_copy(
            src_ref=source.at[block_of(to)],
            dst_ref=target.at[block_of(my)],
            send_sem=send_sem.at[n],
            recv_sem=recv_sem.at[n],
            device_id={"seq": base + to},
            device_id_type=pl.DeviceIdType.MESH,
        )

    def start_all(*args):
        def step(n, carry):
            exchange(n, *args).start()
            return carry

        lax.fori_loop(1, WINDOW, step, 0)

    def wait_all(*args):
        def step(n, carry):
            exchange(n, *args).wait()
            return carry

        lax.fori_loop(1, WINDOW, step, 0)

    stores = []

    def store(source, target):
        copy = pltpu.make_async_copy(source, target, store_sem.at[len(stores)])
        copy.start()
        stores.append(copy)

    lane = lax.broadcasted_iota(jnp.int32, (1, chosen), 1)
    lane_token = lane_tokens(res_ref, chosen, few)
    lane_span = jnp.zeros((1, chosen), jnp.int32)
    for h in range(heads):
        lane_span = jnp.where(lane // few == h, span_ref[h], lane_span)
    row = lax.broadcasted_iota(jnp.int32, (tokens, tokens), 0)
    col = lax.broadcasted_iota(jnp.int32, (tokens, tokens), 1)
    start = me * tokens
    huge = jnp.int32(1 << 20)
    row_ok = row + start < count
    far[...] = jnp.where(row_ok, row ^ col, huge)
    thin = lax.broadcasted_iota(jnp.int32, (chosen, 1), 0)
    thin_res = jnp.zeros((chosen, 1), jnp.int32)
    for h in range(heads):
        thin_res = jnp.where(thin // few == h, res_ref[h], thin_res)
    pick = one_hot(col == (thin % few) * STEP + thin_res)
    own = own_columns(chosen, width, few, dim)

    def picked(n, order, source, keep):
        loads[order].wait()
        part = jnp.where(own, nn(pick, source[...]), 0.0).astype(BF)
        if keep is not None:
            keep[...] = part
        return nn(part, fold_matrix(heads, dim, chosen, n * dim))

    packed = picked(0, 0, q_ref, qb) + picked(3, 1, g_ref, gb)
    packed = packed + picked(1, 2, k_ref, None)
    mask = jnp.where(row_ok, row ^ lane_token, huge) < lane_span
    s = jnp.where(mask, nt(k_ref[...], qb[...]) * scale2, FLOOR)
    top = jnp.max(s, axis=0, keepdims=True)
    p = jnp.exp2(s - top)
    total = jnp.sum(p, axis=0, keepdims=True)
    p = p * (1.0 / total)
    packed = packed + picked(2, 3, v_ref, None)
    dp = nt(v_ref[...], gb[...])
    local_lse = top + jnp.log(total) * LOG2E
    local_delta = jnp.sum(p * dp, axis=0, keepdims=True)
    pb[...] = p
    dpb[...] = dp
    stat_out = stat_matrix(chosen, 4 * dim)
    stats = rows_block(parts_of(local_lse, 3) + parts_of(local_delta, 2), 16, chosen)
    send1[...] = (packed + tn(stats.astype(BF), stat_out)).astype(BF)

    pl.semaphore_wait(barrier, WINDOW - 1)
    start_all(send1, recv1, ss1, rs1)
    recv1[block_of(my), :] = send1[block_of(my), :]
    store(pb, pb_hbm)
    store(dpb, dpb_hbm)
    store(qb, qb_hbm)
    store(gb, gb_hbm)
    for source, target in zip((q_ref, g_ref, k_ref, v_ref), (qt, gt, kt, vt)):
        target[...] = source[...].T

    query_ok = lane + start < count

    def local_head(h, carry):
        at = pl.ds(pl.multiple_of(h * dim, 16), dim)
        qh, kh, vh, gh = qt[at, :], kt[at, :], vt[at, :], gt[at, :]
        s = jnp.where(far[...] < span_ref[h], tn(kh, qh) * scale2, FLOOR)
        top = jnp.max(s, axis=0, keepdims=True)
        p = jnp.exp2(s - top)
        inverse = 1.0 / jnp.sum(p, axis=0, keepdims=True)
        dp = tn(vh, gh)
        delta = jnp.sum(p * dp, axis=0, keepdims=True) * inverse
        keep = query_ok & (lane % STEP != res_ref[h])
        w = p * jnp.where(keep, inverse, 0.0)
        ds = (w * (dp - delta)).astype(BF)
        dqt[at, :] = nn(kh, ds) * scale
        dkt[at, :] = nt(qh, ds) * scale
        dvt[at, :] = nt(gh, w.astype(BF))
        return carry

    lax.fori_loop(0, EARLY_HEADS, local_head, 0, unroll=2)

    wait_all(send1, recv1, ss1, rs1)
    feature_in = lax.broadcasted_iota(jnp.int32, (chosen, chosen), 0)
    feature_out = lax.broadcasted_iota(jnp.int32, (chosen, chosen), 1)

    def moved(source, target):
        shift = feature_in - feature_out == (source - target) * dim
        inside = (feature_out >= target * dim) & (feature_out < (target + 1) * dim)
        return nn(got, one_hot(shift & inside)).astype(BF)

    got = recv1[...]
    kp, qp, gp = moved(1, 0), moved(0, 1), moved(3, 2)
    stats = nt(stat_out, got)
    local_lse = stats[0:1] + stats[1:2] + stats[2:3]
    local_delta = stats[3:4] + stats[4:5]
    limit = count - base * tokens - res_ref[my]
    s = jnp.where(row * STEP < limit, nt(got, qp) * scale2, FLOOR)
    top = jnp.max(s, axis=0, keepdims=True)
    p = jnp.exp2(s - top)
    total = jnp.sum(p, axis=0, keepdims=True)
    dilated_lse = top + jnp.log(total) * LOG2E
    most = jnp.maximum(local_lse, dilated_lse)
    both = most + jnp.log(jnp.exp2(local_lse - most) + jnp.exp2(dilated_lse - most)) * LOG2E
    here_ok = lane * STEP < limit
    local_part = jnp.where(here_ok, jnp.exp2(local_lse - both), 0.0)
    u = p * jnp.where(here_ok, jnp.exp2(top - both), 0.0)
    dp = nt(got, gp)
    delta = local_part * local_delta + jnp.sum(u * dp, axis=0, keepdims=True)
    delta = jnp.where(here_ok, delta, 0.0)
    ds = (u * (dp - delta)).astype(BF)
    stats = rows_block(parts_of(local_part, 2) + parts_of(delta, 2), 16, chosen)
    packed = (tn(ds, kp) + nn(ds, qp)) * scale + nn(u.astype(BF), gp)
    send2[...] = (packed + tn(stats.astype(BF), stat_matrix(chosen, 3 * dim))).astype(BF)
    start_all(send2, recv2, ss2, rs2)
    own_copy = pltpu.make_async_copy(
        send2.at[block_of(my)], recv2.at[block_of(my)], own_sem.at[0]
    )
    own_copy.start()

    lax.fori_loop(EARLY_HEADS, heads, local_head, 0, unroll=2)

    for source, target, output in (
        (dqt, dq_ref, dq_hbm), (dkt, dk_ref, dk_hbm), (dvt, dv_ref, dv_hbm)
    ):
        target[...] = source[...].astype(BF).T
        store(target, output)
    wait_all(send2, recv2, ss2, rs2)
    own_copy.wait()
    for copy in stores:
        copy.wait()


def finish(
    res_ref, back_hbm, pb_hbm, dpb_hbm, k_hbm, dql_hbm, qb_hbm, dkl_hbm, gb_hbm, dvl_hbm,
    dq_hbm, dk_hbm, dv_hbm,
    back, pb, dpb, k_ref, dql, qb, dkl, gb, dvl, dq_ref, dk_ref, dv_ref, load_sem, store_sem,
):
    tokens, width = k_ref.shape
    heads = res_ref.shape[0]
    dim = width // heads
    few = tokens // STEP
    chosen = heads * few
    scale = 1.0 / math.sqrt(dim)
    sources = (back_hbm, pb_hbm, dpb_hbm, k_hbm, dql_hbm, qb_hbm, dkl_hbm, gb_hbm, dvl_hbm)
    targets = (back, pb, dpb, k_ref, dql, qb, dkl, gb, dvl)
    loads = [
        pltpu.make_async_copy(source, target, load_sem.at[n])
        for n, (source, target) in enumerate(zip(sources, targets))
    ]
    for load in loads:
        load.start()
    row = lax.broadcasted_iota(jnp.int32, (tokens, chosen), 0)
    pick = one_hot(row == lane_tokens(res_ref, chosen, few))
    own = own_columns(chosen, width, few, dim)
    stat_in = stat_matrix(chosen, 3 * dim)
    for load in loads[:3]:
        load.wait()
    got = back[...]
    stats = nt(stat_in, got)
    local_part = stats[0:1] + stats[1:2]
    delta = stats[2:3] + stats[3:4]
    w = pb[...] * local_part
    ds = (w * (dpb[...] - delta)).astype(BF)
    w = w.astype(BF)

    def returned(n):
        return nt(got, fold_matrix(heads, dim, chosen, n * dim))

    def spread(x):
        return nn(pick, jnp.where(own, x, 0.0).astype(BF))

    def put(n, block, target, x):
        block[...] = x.astype(BF)
        copy = pltpu.make_async_copy(block, target, store_sem.at[n])
        copy.start()
        return copy

    dk_far, dv_far = spread(returned(1)), spread(returned(2))
    loads[3].wait()
    dq = spread(tn(ds, k_ref[...]) * scale + returned(0))
    loads[4].wait()
    stores = [put(0, dq_ref, dq_hbm, dql[...].astype(F32) + dq)]
    loads[5].wait()
    dk = nn(ds, qb[...]) * scale + dk_far
    loads[6].wait()
    stores.append(put(1, dk_ref, dk_hbm, dkl[...].astype(F32) + dk))
    loads[7].wait()
    dv = nn(w, gb[...]) + dv_far
    loads[8].wait()
    stores.append(put(2, dv_ref, dv_hbm, dvl[...].astype(F32) + dv))
    for copy in stores:
        copy.wait()


def shards(queries, keys, values, grad_out, local_span, head_residue, valid_count):
    tokens, width = queries.shape
    heads = local_span.shape[0]
    chosen = heads * (tokens // STEP)
    assert heads == WINDOW and chosen == tokens
    smem = pl.BlockSpec(memory_space=pltpu.SMEM)
    hbm = pl.BlockSpec(memory_space=pltpu.MemorySpace.HBM)
    full = ((tokens, width), BF)
    turned = ((width, tokens), BF)
    pair = ((tokens, chosen), F32)
    block = ((chosen, chosen), BF)
    out = jax.ShapeDtypeStruct(*full)
    between = (block, pair, pair, full, full, full, full, full)
    back, pb, dpb, qb, gb, dql, dkl, dvl = pl.pallas_call(
        kernel,
        out_shape=tuple(jax.ShapeDtypeStruct(*x) for x in between),
        in_specs=[smem] * 3 + [hbm] * 4,
        out_specs=(hbm,) * 8,
        scratch_shapes=[pltpu.VMEM(*full)] * 4
        + [
            pltpu.SemaphoreType.DMA((4,)),
            pltpu.SemaphoreType.DMA((7,)),
            pltpu.SemaphoreType.DMA((1,)),
        ]
        + [pltpu.VMEM(*turned)] * 4
        + [pltpu.VMEM((width, tokens), F32)] * 3
        + [pltpu.VMEM(*full)] * 5
        + [pltpu.VMEM((tokens, tokens), jnp.int32)]
        + [pltpu.VMEM(*pair)] * 2
        + [pltpu.VMEM(*block)] * 3
        + [pltpu.SemaphoreType.DMA((WINDOW,))] * 4,
        compiler_params=pltpu.CompilerParams(
            collective_id=0, has_side_effects=True, vmem_limit_bytes=VMEM_LIMIT
        ),
    )(local_span, head_residue, valid_count, queries, keys, values, grad_out)
    return pl.pallas_call(
        finish,
        out_shape=(out, out, out),
        in_specs=[smem] + [hbm] * 9,
        out_specs=(hbm, hbm, hbm),
        scratch_shapes=[pltpu.VMEM(*block), pltpu.VMEM(*pair), pltpu.VMEM(*pair)]
        + [pltpu.VMEM(*full)] * 9
        + [pltpu.SemaphoreType.DMA((9,)), pltpu.SemaphoreType.DMA((3,))],
        compiler_params=pltpu.CompilerParams(vmem_limit_bytes=VMEM_LIMIT),
    )(head_residue, back, pb, dpb, keys, dql, qb, dkl, gb, dvl)


def solution(mesh):
    rows = P(("groups", "seq"), None)
    return jax.shard_map(
        shards,
        mesh=mesh,
        in_specs=(rows, rows, rows, rows, P(), P(), P("groups")),
        out_specs=(rows, rows, rows),
        check_vma=False,
    )
```

time: 26.4 us -> 25.6 us (0.970)
  local copies, waits for them, and re-layouts: 6.22 us -> 0 us
  Pallas kernels: 18.6 us -> 24.1 us
    unnamed x15 -> x0, local copies, waits for them, and re-layouts: 6.22 us -> none
    pallas_call x1 -> x2, Pallas kernels: 18.6 us -> 24.1 us  [the longest x1 19.4 us: shards(): pl.pallas_call(kernel, out_shape=tuple((jax.ShapeDtypeStruct(*x) for x in...]
where the time goes in v3:
time: 25.6 us; the launch traced here: 25.4 us
  Pallas kernels  24.1 us (94%)
  between operations  1.29 us (5%)
    pallas_call x1, Pallas kernels, shards(): pl.pallas_call(kernel, out_shape=tuple((jax.ShapeDtypeStruct(*x) for x in...  19.4 us
    pallas_call x1, Pallas kernels, shards(): pl.pallas_call(finish, out_shape=(out, out, out), in_specs=[smem] + [hbm]...  4.73 us

profile of v3, /device:TPU:0, one launch (start us, length us, event | category | flops | bytes accessed | tf_op | source)
XLA Modules:
  0.0 25.4 jit_solution(5419222432377987117)
XLA Ops:
  1.3 19.4 %shard_map.94 = (bf16[256,256]{1,0:T(8,128)(2,1)}, f32[256,256]{1,0:T(8,128)}, f32[256,256]{1,0:T(8,128)}, bf16[256,768]{1,0:T(8,128)(2,1)}, bf16[256,768]{1,0:T...) custom-call(s32[16]{0:T(128)} %span_ref.1, s32[16]{0:T(128)} %res_ref.3, ...), custom_call_target="tpu_custom_call" | custom-call | tf_op jit(solution)/shard_map/pallas_call | solution.py:356
  20.7 4.7 %shard_map.95 = (bf16[256,768]{1,0:T(8,128)(2,1)}, bf16[256,768]{1,0:T(8,128)(2,1)}, bf16[256,768]{1,0:T(8,128)(2,1)}) custom-call(s32[16]{0:T(128)} %res_ref.3, bf16[256,256]{1,0:T(8,128)(2,1)} %get-tuple-element.11.back_hbm, f32[256,256]{1,0:T(8,128)} %get-tuple-element.12.pb_hbm, f32[256,256]{1,0:T(8,128)} %get-tuple-element.13.dpb_hbm, ...), custom_call_target="tpu_custom_call" | custom-call | tf_op jit(solution)/shard_map/pallas_call | solution.py:378

commit v4 on v2

--- a/solution.py
+++ b/solution.py
@@ -11,7 +11,7 @@
 WINDOW = 16
 FLOOR = -1e30
 LOG2E = 1.4426950408889634
-EARLY_HEADS = 6
+EARLY_HEADS = 8
 VMEM_LIMIT = 63 * 2**20
 
 BF = jnp.bfloat16
@@ -111,7 +111,14 @@
 
     def wait_all(*args):
         def step(n, carry):
-            exchange(n, *args).wait()
+            exchange(n, *args).wait_recv()
+            return carry
+
+        lax.fori_loop(1, WINDOW, step, 0)
+
+    def wait_sent(*args):
+        def step(n, carry):
+            exchange(n, *args).wait_send()
             return carry
 
         lax.fori_loop(1, WINDOW, step, 0)
@@ -192,7 +199,7 @@
         dvt[at, :] = nt(gh, w.astype(BF))
         return carry
 
-    lax.fori_loop(0, EARLY_HEADS, local_head, 0, unroll=2)
+    lax.fori_loop(0, EARLY_HEADS, local_head, 0, unroll=4)
 
     wait_all(send1, recv1, ss1, rs1)
     got = recv1[...].astype(F32).T
@@ -225,7 +232,7 @@
     start_all(send2, recv2, ss2, rs2)
     recv2[block_of(my), :] = send2[block_of(my), :]
 
-    lax.fori_loop(EARLY_HEADS, heads, local_head, 0, unroll=2)
+    lax.fori_loop(EARLY_HEADS, heads, local_head, 0, unroll=4)
 
     wait_all(send2, recv2, ss2, rs2)
     back = recv2[...].astype(F32).T
@@ -257,6 +264,8 @@
     dv = dvt[...] + nt(gb[...], w.astype(BF)) + spread(lambda h: dv_few)
     dv_ref[...] = dv.astype(BF)
     store_dv = store(2, dv_ref, dv_hbm)
+    wait_sent(send1, recv1, ss1, rs1)
+    wait_sent(send2, recv2, ss2, rs2)
     store_dq.wait()
     store_dk.wait()
     store_dv.wait()

time: 23.2 us -> 23.2 us (level)
  no operation moved by 1% of the time
where the time goes in v4:
time: 23.2 us; the launch traced here: 23 us
  Pallas kernels  21.7 us (94%)
  between operations  1.29 us (6%)
    pallas_call x1, Pallas kernels, shards(): pl.pallas_call(kernel, out_shape=(turned, turned, turned), in_specs=[smem...  19.4 us
    pallas_call x1, Pallas kernels, shards(): pl.pallas_call(finish, out_shape=(out, out, out), in_specs=[hbm] * 3, out...  2.26 us

profile of v4, /device:TPU:0, one launch (start us, length us, event | category | flops | bytes accessed | tf_op | source)
XLA Modules:
  0.0 23.0 jit_solution(10696613331278685311)
XLA Ops:
  1.3 19.4 %shard_map.94 = (bf16[768,256]{1,0:T(8,128)(2,1)}, bf16[768,256]{1,0:T(8,128)(2,1)}, bf16[768,256]{1,0:T(8,128)(2,1)}) custom-call(s32[16]{0:T(128)} %span_ref.1, s32[16]{0:T(128)} %res_ref.1, s32[1]{0:T(128)S(6)} %copy.10.count_ref, bf16[256,768]{1,0:T(8,128)(2,1)} %q_hbm.1, bf16[256,768]{1,0:T(8,128)(2,1)} %k_hbm.1, bf16[256,768]{1,0:T(8,128)(2,1)} %v_hbm.1, ...), custom_call_target="tpu_custom_call" | custom-call | tf_op jit(solution)/shard_map/pallas_call | solution.py:303
  20.7 2.3 %shard_map.95 = (bf16[256,768]{1,0:T(8,128)(2,1)}, bf16[256,768]{1,0:T(8,128)(2,1)}, bf16[256,768]{1,0:T(8,128)(2,1)}) custom-call(bf16[768,256]{1,0:T(8,128)(2,1)} %get-tuple-element.6.a_in, bf16[768,256]{1,0:T(8,128)(2,1)} %get-tuple-element.7.b_in, bf16[768,256]{1,0:T(8,128)(2,1)} %get-tuple-element.8.c_in), custom_call_target="tpu_custom_call" | custom-call | tf_op jit(solution)/shard_map/pallas_call | solution.py:327
